TPU v7x, 512 devices: a whole 4x8x8 slice. The times are simulated.
512 devices in a mesh: sub: 128 (over y, z, core), freq: 4 (over x).
Axes of the slice: x: 4, y: 8, z: 8, core: 2. Of those that a mesh axis runs over, the one named last changes fastest.
Arguments:
- response: bfloat16 [4, 1536, 96, 256], P('freq', 'sub'), may hold values from -6 to 6
- measured: bfloat16 [4, 12288, 256], P('freq', 'sub'), may hold values from -6 to 6
- sensor_owner: int32 [12288], P('sub'), may hold values from 0 to 127, as said below
- sensor_row: int32 [12288], P('sub'), may hold values from 0 to 1151
- adj_diag: bfloat16 [4, 1536, 2, 96, 96], P('freq', 'sub')
- adj_off: bfloat16 [4, 1536, 5, 2, 96, 96], P('freq', 'sub')
- block_cols: int32 [1536, 5], P('sub'), may hold values from 0 to 13, as said below
- precond: bfloat16 [4, 1536, 2, 96, 96], P('freq', 'sub')
- stiff_deriv: bfloat16 [1536, 96, 96], P('sub'), may hold values from -0.625 to 0.625
Outputs:
- adjoint: bfloat16 [4, 1536, 96, 256], P('freq', 'sub')
- gradient: float32 [1536], P('sub')
Inputs may be any that keep to these rules, and one draw needn't show every extreme that they name: `sensor_owner`: among the 96 channels held by one index of sub, no subdomain is named more than 3 times, and one subdomain is named exactly 3 times by the channels of every index of sub. `block_cols`: in every subdomain some block row has a coupling tile with column 0 and some has one with column 13.
All inputs are finite; a program needn't handle non-finite values.
Results may differ from a plain program's by a relative error of at most 0.0061.
Values may be sent and summed in bfloat16 or wider, within the bound.
No kernel may reach another device: no remote copies, remote signals or barrier semaphores. Data moves between devices by JAX's collectives and lax.ppermute only.
A program may use at most 64 MiB of HBM per device.

v0:
```python
import math

import jax
import jax.numpy as jnp
from jax import lax
from jax.sharding import PartitionSpec as P

SWEEPS = 3


def with_halo(block, sides, width):
    for axis, dim in sides:
        count = lax.axis_size(axis)
        forward = [(i, i + 1) for i in range(count - 1)]
        backward = [(target, source) for source, target in forward]
        low = lax.ppermute(
            lax.slice_in_dim(block, block.shape[dim] - width, None, axis=dim), axis, forward
        )
        high = lax.ppermute(lax.slice_in_dim(block, 0, width, axis=dim), axis, backward)
        block = jnp.concatenate([low, block, high], axis=dim)
    return block


def complex_apply(tile_set, vectors):
    column_half = vectors.shape[-1] // 2
    real_part = jnp.einsum(
        "bij,bjn->bin", tile_set[:, 0], vectors, preferred_element_type=jnp.float32
    )
    imag_part = jnp.einsum(
        "bij,bjn->bin", tile_set[:, 1], vectors, preferred_element_type=jnp.float32
    )
    return jnp.concatenate(
        [
            real_part[..., :column_half] - imag_part[..., column_half:],
            real_part[..., column_half:] + imag_part[..., :column_half],
        ],
        axis=-1,
    )


def coupled_apply(tile_set, gathered):
    column_half = gathered.shape[-1] // 2
    real_part = jnp.einsum(
        "bkij,bkjn->bin", tile_set[:, :, 0], gathered, preferred_element_type=jnp.float32
    )
    imag_part = jnp.einsum(
        "bkij,bkjn->bin", tile_set[:, :, 1], gathered, preferred_element_type=jnp.float32
    )
    return jnp.concatenate(
        [
            real_part[..., :column_half] - imag_part[..., column_half:],
            real_part[..., column_half:] + imag_part[..., :column_half],
        ],
        axis=-1,
    )


def shards(
    response,
    measured,
    sensor_owner,
    sensor_row,
    adj_diag,
    adj_off,
    block_cols,
    precond,
    stiff_deriv,
):
    own_resp = response[0]
    block_count, rows_per, col_count = own_resp.shape
    flat_resp = own_resp.reshape(block_count * rows_per, col_count)
    local_measurements = measured[0]
    my_index = lax.axis_index("sub")
    empty_load = jnp.zeros((block_count * rows_per, col_count), jnp.float32)
    incoming_rows = lax.all_gather(local_measurements, "sub", axis=0, tiled=True)
    owners_in = lax.all_gather(sensor_owner, "sub", axis=0, tiled=True)
    index_in = lax.all_gather(sensor_row, "sub", axis=0, tiled=True)
    owned = owners_in == my_index
    safe_index = jnp.where(owned, index_in, 0)
    predicted = flat_resp[safe_index].astype(jnp.float32)
    misfit = jnp.where(owned[:, None], predicted - incoming_rows.astype(jnp.float32), 0.0)
    load_flat = empty_load.at[safe_index].add(misfit)
    load_rhs = load_flat.reshape(block_count, rows_per, col_count)
    diag_tiles = adj_diag[0]
    off_tiles = adj_off[0]
    prec_tiles = precond[0]
    adjoint = complex_apply(prec_tiles, load_rhs.astype(jnp.bfloat16))
    for jacobi_sweep_step in range(SWEEPS - 1):
        iterate = adjoint.astype(jnp.bfloat16)
        extended = with_halo(iterate, (("sub", 0),), 1)
        gathered = extended[block_cols]
        applied = complex_apply(diag_tiles, iterate) + coupled_apply(off_tiles, gathered)
        update = (load_rhs - applied).astype(jnp.bfloat16)
        adjoint = adjoint + complex_apply(prec_tiles, update)
    stiff_resp = jnp.einsum(
        "bij,bjn->bin", stiff_deriv, own_resp, preferred_element_type=jnp.float32
    )
    grad_scale = 1.0 / math.sqrt(rows_per * col_count)
    partial_grad = jnp.sum(adjoint * stiff_resp, axis=(1, 2)) * grad_scale
    gradient = lax.psum(partial_grad, "freq")
    return (adjoint.astype(jnp.bfloat16)[None], gradient)


def solution(mesh):
    in_specs = (
        P("freq", "sub", None, None),
        P("freq", "sub", None),
        P("sub"),
        P("sub"),
        P("freq", "sub", None, None, None),
        P("freq", "sub", None, None, None, None),
        P("sub", None),
        P("freq", "sub", None, None, None),
        P("sub", None, None),
    )
    out_specs = (P("freq", "sub", None, None), P("sub"))
    return jax.shard_map(shards, mesh=mesh, in_specs=in_specs, out_specs=out_specs, check_vma=False)
```

profile of v0, /device:TPU:32, one launch (start us, length us, event | category | flops | bytes accessed | tf_op | source)
XLA Modules:
  0.0 479.8 jit_solution(6568776765771460536)
XLA Ops:
  7.2 1.4 dynamic-slice
  13.3 1.1 copy.27
  14.5 4.1 copy.26
  18.6 174.8 %all-reduce.5.cloned.1.call-done = (s32[12288]{0:T(1024)}, s32[12288]{0:T(1024)}) async-done(((s32[12288]{0:T(1024)}, s32[12288]{0:T(1024)}), (s32[12288]{0:T(1024)}, s32[12288]{0:T(1024)})) %all-reduce.5.cloned.1.call-update) | async-done | bytes 98320
  194.2 84.5 %all-gather.3.cloned.1.call-done = bf16[1,12288,256]{2,1,0:T(8,128)(2,1)} async-done(((bf16[1,96,256]{2,1,0:T(8,128)(2,1)}), bf16[1,12288,256]{2,1,0:T(8,128)(2,1)}) %all-gather.3.cloned.1.call-update) | async-done | bytes 6291472 | tf_op jit(solution)/shard_map/all_gather | solution.py:75
  278.7 131.1 %scatter_custom_fusion = f32[1152,256]{1,0:T(8,128)S(1)} fusion(s32[12288]{0:T(1024)S(1)} %get-tuple-element.5, bf16[1,12288,256]{2,1,0:T(8,128)(2,1)} %all-gather.3.cloned.1.call-done, f32[]{:T(128)} %constant.7.clone.1, pred[12288]{0:T(1024)(128)(4,1)S(1)} %get-tuple-element.6, bf16[1152,256]{1,0:T(8,128)(2,1)S(1)} %bitcast.108, ...), kind=kCustom, calls=%fused_computation.6 | custom fusion | flops 15728640 | bytes 8123392 | tf_op jit(solution)/shard_map/scatter-add | solution.py:82
  411.6 2.2 collective-permute-start
  413.8 6.7 %collective-permute-start.1 = (bf16[1,96,256]{2,1,0:T(8,128)(2,1)S(1)}, bf16[1,96,256]{2,1,0:T(8,128)(2,1)S(1)}, u32[]{:S(2)}, u32[]{:S(2)}) collective-permute-start(bf16[1,96,256]{2,1,0:T(8,128)(2,1)S(1)} %get-tuple-element.24), channel_id=1, source_target_pairs={{4,0},{8,4},{12,8},{16,12},{20,16},{24,20},{28,24},{32,28},{36,32}... | collective-permute-start | bytes 147464 | tf_op jit(solution)/shard_map/ppermute | solution.py:19
  420.5 1.1 slice_subtract_fusion.5
  422.4 2.4 gather_fusion
  424.7 3.1 convolution_bitcast_fusion.8
  427.9 2.5 convolution_bitcast_fusion.9
  430.5 0.9 copy-done.18
  433.5 0.9 copy-done.4
  436.1 1.9 collective-permute-start.2
  438.0 7.2 %collective-permute-start.3 = (bf16[1,96,256]{2,1,0:T(8,128)(2,1)S(1)}, bf16[1,96,256]{2,1,0:T(8,128)(2,1)S(1)}, u32[]{:S(2)}, u32[]{:S(2)}) collective-permute-start(bf16[1,96,256]{2,1,0:T(8,128)(2,1)S(1)} %get-tuple-element.22), channel_id=1, source_target_pairs={{4,0},{8,4},{12,8},{16,12},{20,16},{24,20},{28,24},{32,28},{36,32}... | collective-permute-start | bytes 147464 | tf_op jit(solution)/shard_map/ppermute | solution.py:19
  445.2 1.2 slice_subtract_fusion.2
  446.8 2.4 gather_fusion.1
  449.2 3.1 convolution_bitcast_fusion.2
  452.3 2.5 convolution_bitcast_fusion.3
  455.0 0.9 copy-done.16
  458.0 0.9 copy-done.5
  459.9 10.9 %psum.7 = f32[12]{0:T(128)} all-reduce(f32[12]{0:T(128)S(1)} %broadcast_multiply_fusion), channel_id=1, replica_groups=mesh['sub'=128,'freq'=4] {'freq'}, use_global_device_ids=true, to_apply=%region_2.3 | all-reduce | flops 12 | bytes 96 | tf_op jit(solution)/shard_map/psum | solution.py:100
  470.8 2.1 fusion.9
  (87 shorter events, 15.0 us)
Async XLA Ops:
  7.2 271.5 %copy-start = (bf16[1,12,96,256]{3,2,1,0:T(8,128)(2,1)S(1)}, bf16[1,12,96,256]{3,2,1,0:T(8,128)(2,1)}, u32[]{:S(2)}) copy-start(bf16[1,12,96,256]{3,2,1,0:T(8,128)(2,1)} %param.9) | copy-start | bytes 1769476
  7.2 7.2 %copy-start.20 = (bf16[1,12,2,96,96]{4,3,2,1,0:T(8,128)(2,1)S(1)}, bf16[1,12,2,96,96]{4,3,2,1,0:T(8,128)(2,1)}, u32[]{:S(2)}) copy-start(bf16[1,12,2,96,96]{4,3,2,1,0:T(8,128)(2,1)} %param.16) | copy-start | bytes 1327108
  7.2 186.2 %all-reduce.5.cloned.1.call-start = ((), (), s32[]{:S(2)}) async-start(), calls=%async_computation.1 | async-start | bytes 196608
  11.7 267.0 %all-gather.3.cloned.1.call-start = ((), (), s32[]{:S(2)}) async-start(), calls=%async_computation | async-start | bytes 6340608 | tf_op jit(solution)/shard_map/all_gather | solution.py:75
  14.4 396.5 %copy-start.14 = (bf16[1,12,2,96,96]{4,3,1,2,0:T(8,128)(2,1)}, bf16[1,12,2,96,96]{4,3,1,2,0:T(8,128)(2,1)S(1)}, u32[]{:S(2)}) copy-start(bf16[1,12,2,96,96]{4,3,1,2,0:T(8,128)(2,1)S(1)} %copy.27) | copy-start | bytes 1327108
  14.5 395.6 %copy-start.10 = (bf16[1,12,2,96,96]{4,3,1,2,0:T(8,128)(2,1)}, bf16[1,12,2,96,96]{4,3,1,2,0:T(8,128)(2,1)S(1)}, u32[]{:S(2)}) copy-start(bf16[1,12,2,96,96]{4,3,1,2,0:T(8,128)(2,1)S(1)} %copy.28) | copy-start | bytes 1327108
  411.6 10.1 %collective-permute-start = (bf16[1,96,256]{2,1,0:T(8,128)(2,1)S(1)}, bf16[1,96,256]{2,1,0:T(8,128)(2,1)S(1)}, u32[]{:S(2)}, u32[]{:S(2)}) collective-permute-start(bf16[1,96,256]{2,1,0:T(8,128)(2,1)S(1)} %get-tuple-element.23), channel_id=1, source_target_pairs={{0,4},{4,8},{8,12},{12,16},{16,20},{20,24},{24,28},{28,32},{32,36}... | collective-permute-start | bytes 147464 | tf_op jit(solution)/shard_map/ppermute | solution.py:16
  413.8 8.4 %collective-permute-start.1 = (bf16[1,96,256]{2,1,0:T(8,128)(2,1)S(1)}, bf16[1,96,256]{2,1,0:T(8,128)(2,1)S(1)}, u32[]{:S(2)}, u32[]{:S(2)}) collective-permute-start(bf16[1,96,256]{2,1,0:T(8,128)(2,1)S(1)} %get-tuple-element.24), channel_id=1, source_target_pairs={{4,0},{8,4},{12,8},{16,12},{20,16},{24,20},{28,24},{32,28},{36,32}... | collective-permute-start | bytes 147464 | tf_op jit(solution)/shard_map/ppermute | solution.py:19
  424.7 3.2 copy-start.1
  430.4 1.1 copy-start.18
  430.4 1.2 copy-start.19
  433.3 1.1 copy-start.4
  433.5 1.1 copy-start.6
  433.5 1.1 copy-start.8
  436.1 10.3 %collective-permute-start.2 = (bf16[1,96,256]{2,1,0:T(8,128)(2,1)S(1)}, bf16[1,96,256]{2,1,0:T(8,128)(2,1)S(1)}, u32[]{:S(2)}, u32[]{:S(2)}) collective-permute-start(bf16[1,96,256]{2,1,0:T(8,128)(2,1)S(1)} %get-tuple-element.21), channel_id=1, source_target_pairs={{0,4},{4,8},{8,12},{12,16},{16,20},{20,24},{24,28},{28,32},{32,36}... | collective-permute-start | bytes 147464 | tf_op jit(solution)/shard_map/ppermute | solution.py:16
  438.0 8.7 %collective-permute-start.3 = (bf16[1,96,256]{2,1,0:T(8,128)(2,1)S(1)}, bf16[1,96,256]{2,1,0:T(8,128)(2,1)S(1)}, u32[]{:S(2)}, u32[]{:S(2)}) collective-permute-start(bf16[1,96,256]{2,1,0:T(8,128)(2,1)S(1)} %get-tuple-element.22), channel_id=1, source_target_pairs={{4,0},{8,4},{12,8},{16,12},{20,16},{24,20},{28,24},{32,28},{36,32}... | collective-permute-start | bytes 147464 | tf_op jit(solution)/shard_map/ppermute | solution.py:19
  449.2 3.2 copy-start.2
  454.8 1.1 copy-start.16
  454.9 1.2 copy-start.17
  457.8 1.1 copy-start.5
  457.8 1.4 copy-start.7
  457.8 1.6 copy-start.9
  457.8 1.7 copy-start.21
  457.9 2.0 copy-start.13
  (6 other events, 5.5 us)
Sparse Core Ops, SparseCore 0:
  12.0 181.2 all-reduce.4
  196.5 82.1 all-gather.2
where the time goes:
time: 481 us; the launch traced here: 480 us
  waiting for transfers between devices  261 us (54%)
  other arithmetic  139 us (29%)
  local copies, waits for them, and re-layouts  21.4 us (4%)
  starting transfers between devices  18.1 us (4%)
  between operations  15.1 us (3%)
  matrix products  14.6 us (3%)
  blocking collectives  10.9 us (2%)
    unnamed x3, waiting for transfers between devices  175 us
    scatter-add x1, other arithmetic, shards(): load_flat = empty_load.at[safe_index].add(misfit)  131 us
    all_gather x1, waiting for transfers between devices, shards(): lax.all_gather(local_measurements, 'sub', axis=0, tiled=True)  84.5 us
    unnamed x56, local copies, waits for them, and re-layouts  16.5 us
    ppermute x2, starting transfers between devices, with_halo(): lax.ppermute(lax.slice_in_dim(block, 0, width, axis=dim), axis, backward)  13.9 us
    psum x1, blocking collectives, shards(): gradient = lax.psum(partial_grad, 'freq')  10.9 us
  transfers between devices with their start and end apart: 6, of which 4 were waited for; matrix products, arithmetic and copies ran while one was open for 2% of the time, Pallas kernels for 0%

commit v1 on v0

v1 whole, which is shorter than its diff:
```python
import functools
import math

import jax
import jax.numpy as jnp
from jax import lax
from jax.experimental import pallas as pl
from jax.experimental.pallas import tpu as pltpu
from jax.sharding import PartitionSpec as P

SLOTS = 4
VMEM_LIMIT = 48 * 1024 * 1024

F32 = jnp.float32
BF16 = jnp.bfloat16


def iota(shape, dim):
    return lax.broadcasted_iota(jnp.int32, shape, dim)


def complex_product(tile_pair, block):
    _, m, depth = tile_pair.shape
    half = block.shape[-1] // 2
    both = jnp.dot(tile_pair.reshape(2 * m, depth), block, preferred_element_type=F32)
    return combine(both, m, half)


def combine(both, m, half):
    real_part = both[:m, :half] - both[m:, half:]
    imag_part = both[:m, half:] + both[m:, :half]
    return real_part, imag_part


def pack_kernel(rows_per, owner_ref, row_ref, measured_ref, out_ref):
    count = measured_ref.shape[0]
    slots_all = out_ref.shape[0]
    owner = owner_ref[...]
    row = row_ref[...]
    code = (owner * 2048 + row).astype(F32)
    lanes = jnp.broadcast_to(jnp.pad(code, ((0, 0), (0, 128 - count))), (128, 128))
    code_col = jnp.transpose(lanes)[:count, :count].astype(jnp.int32)
    owner_col = code_col >> 11
    row_col = code_col & 2047
    same = jnp.broadcast_to(owner, (count, count)) == owner_col
    sub = iota((count, count), 0)
    lane = iota((count, count), 1)
    rank_row = jnp.sum(jnp.where(same & (sub < lane), 1, 0), axis=0, keepdims=True)
    rank_col = jnp.sum(jnp.where(same & (lane < sub), 1, 0), axis=1, keepdims=True)
    place = iota((slots_all, count), 0)
    here = (place >> 2) == owner
    slot = place & 3
    pick = jnp.where(here & (slot == rank_row), 1.0, 0.0).astype(BF16)
    tell = jnp.where(here & (slot == SLOTS - 1), 1.0, 0.0).astype(BF16)
    width = iota((count, 128), 1)
    row_wide = jnp.broadcast_to(row_col[:, :1], (count, 128))
    block = row_wide // rows_per
    inner = row_wide - block * rows_per
    numbers = jnp.where(width == rank_col, block + 1, 0) + jnp.where(
        width == rank_col + SLOTS, inner, 0
    )
    numbers = numbers.astype(F32).astype(BF16)
    rows = jnp.dot(pick, measured_ref[...], preferred_element_type=F32)
    told = jnp.dot(tell, numbers, preferred_element_type=F32)
    half = rows.shape[-1] // 2
    out_ref[:, :half] = (rows[:, :half] + told).astype(BF16)
    out_ref[:, half:] = rows[:, half:].astype(BF16)


def load_kernel(recv_ref, resp_ref, prec_ref, load_ref, lam_ref, it_ref, first_ref, last_ref, place_ref):
    nb, m, cols = resp_ref.shape
    half = cols // 2
    places = recv_ref.shape[0]
    recv = recv_ref[...]
    turned = jnp.transpose(recv[:, :half].astype(F32)).astype(BF16)
    lane = iota((m, half), 1)
    slot = iota((m, places), 1) & 3
    where_row = jnp.full((m, places), -1.0, F32)
    for s in range(SLOTS - 1):
        weights = jnp.where(lane == s, m, 0) + jnp.where(lane == s + SLOTS, 1, 0)
        told = jnp.dot(weights.astype(F32).astype(BF16), turned, preferred_element_type=F32)
        told = pltpu.roll(told, places + s - (SLOTS - 1), 1)
        where_row = jnp.where(slot == s, told - m, where_row)
    place_ref[...] = where_row.astype(jnp.int32) - iota((m, places), 0)
    ones = jnp.ones((places, half), BF16)

    def one(b):
        hit = jnp.where(place_ref[...] == b * m, 1.0, 0.0).astype(BF16)
        summed = jnp.dot(hit, recv, preferred_element_type=F32)
        number = jnp.dot(hit, ones, preferred_element_type=F32)
        resp = resp_ref[b].astype(F32)
        load_re = number * resp[:, :half] - summed[:, :half]
        load_im = number * resp[:, half:] - summed[:, half:]
        load = jnp.concatenate([load_re, load_im], axis=1)
        load_ref[b] = load
        lam_re, lam_im = complex_product(prec_ref[b], load.astype(BF16))
        lam = jnp.concatenate([lam_re, lam_im], axis=1)
        lam_ref[b] = lam
        it_ref[b] = lam.astype(BF16)

    pl.loop(0, nb)(one)
    first_ref[...] = it_ref[0]
    last_ref[...] = it_ref[nb - 1]


def sweep_block(b, cols_ref, ext_ref, load_ref, lam_ref, diag_ref, off_ref, prec_ref):
    _, m, cols = load_ref.shape
    half = cols // 2
    near = off_ref.shape[1]
    both = jnp.dot(diag_ref[b].reshape(2 * m, m), ext_ref[b + 1], preferred_element_type=F32)
    for k in range(near):
        g = cols_ref[b * near + k]
        both += jnp.dot(off_ref[b, k].reshape(2 * m, m), ext_ref[g], preferred_element_type=F32)
    applied_re, applied_im = combine(both, m, half)
    load = load_ref[b]
    update = jnp.concatenate(
        [load[:, :half] - applied_re, load[:, half:] - applied_im], axis=1
    ).astype(BF16)
    step_re, step_im = complex_product(prec_ref[b], update)
    return lam_ref[b] + jnp.concatenate([step_re, step_im], axis=1)


def fill_ext(ext_ref, it_ref, low_ref, high_ref):
    nb = it_ref.shape[0]
    ext_ref[0] = low_ref[...]
    ext_ref[nb + 1] = high_ref[...]
    ext_ref[1 : nb + 1] = it_ref[...]


def sweep_kernel(
    cols_ref, it_ref, low_ref, high_ref, load_ref, lam_ref, diag_ref, off_ref, prec_ref,
    lam_out, it_out, first_ref, last_ref, ext_ref,
):
    nb = load_ref.shape[0]
    fill_ext(ext_ref, it_ref, low_ref, high_ref)

    def one(b):
        lam = sweep_block(b, cols_ref, ext_ref, load_ref, lam_ref, diag_ref, off_ref, prec_ref)
        lam_out[b] = lam
        it_out[b] = lam.astype(BF16)

    pl.loop(0, nb)(one)
    first_ref[...] = it_out[0]
    last_ref[...] = it_out[nb - 1]


def last_kernel(
    scale, cols_ref, it_ref, low_ref, high_ref, load_ref, lam_ref, diag_ref, off_ref, prec_ref,
    stiff_ref, resp_ref, adj_out, grad_out, ext_ref,
):
    nb = load_ref.shape[0]
    fill_ext(ext_ref, it_ref, low_ref, high_ref)
    grad_out[...] = jnp.zeros_like(grad_out)

    def one(b):
        lam = sweep_block(b, cols_ref, ext_ref, load_ref, lam_ref, diag_ref, off_ref, prec_ref)
        adj_out[b] = lam.astype(BF16)
        stiff_resp = jnp.dot(stiff_ref[b], resp_ref[b], preferred_element_type=F32)
        total = jnp.sum(lam * stiff_resp, axis=(0, 1), keepdims=True) * scale
        grad_out[...] += jnp.where(iota(grad_out.shape, 1) == b, total, 0.0)

    pl.loop(0, nb)(one)


def vmem(count):
    return [pl.BlockSpec(memory_space=pltpu.VMEM)] * count


def call(kernel, outs, n_in, smem=0, scratch=()):
    return pl.pallas_call(
        kernel,
        out_shape=outs,
        in_specs=[pl.BlockSpec(memory_space=pltpu.SMEM)] * smem + vmem(n_in),
        out_specs=tuple(vmem(len(outs))) if isinstance(outs, tuple) else vmem(1)[0],
        scratch_shapes=list(scratch),
        compiler_params=pltpu.CompilerParams(vmem_limit_bytes=VMEM_LIMIT),
    )


def halo(first, last, axis):
    count = lax.axis_size(axis)
    forward = [(i, i + 1) for i in range(count - 1)]
    backward = [(i + 1, i) for i in range(count - 1)]
    return lax.ppermute(last, axis, forward), lax.ppermute(first, axis, backward)


def shards(
    response, measured, sensor_owner, sensor_row, adj_diag, adj_off, block_cols, precond, stiff_deriv
):
    resp = response[0]
    diag, off, prec = adj_diag[0], adj_off[0], precond[0]
    nb, m, cols = resp.shape
    peers = lax.axis_size("sub")
    sensors = sensor_owner.shape[0]
    shape = jax.ShapeDtypeStruct
    packed = call(functools.partial(pack_kernel, m), shape((peers * SLOTS, cols), BF16), 3)(
        sensor_owner.reshape(1, sensors), sensor_row.reshape(1, sensors), measured[0]
    )
    recv = lax.all_to_all(packed.reshape(peers, SLOTS, cols), "sub", 0, 0, tiled=True)
    recv = recv.reshape(peers * SLOTS, cols)
    whole32, whole16 = shape((nb, m, cols), F32), shape((nb, m, cols), BF16)
    edge = shape((m, cols), BF16)
    load, lam, it, first, last = call(
        load_kernel, (whole32, whole32, whole16, edge, edge), 3, 0,
        [pltpu.VMEM((m, peers * SLOTS), jnp.int32)],
    )(
        recv, resp, prec
    )
    low, high = halo(first, last, "sub")
    near = block_cols.reshape(-1)
    ext = [pltpu.VMEM((nb + 2, m, cols), BF16)]
    lam, it, first, last = call(sweep_kernel, (whole32, whole16, edge, edge), 8, 1, ext)(
        near, it, low, high, load, lam, diag, off, prec
    )
    low, high = halo(first, last, "sub")
    scale = 1.0 / math.sqrt(m * cols)
    adjoint, grad = call(
        functools.partial(last_kernel, scale), (whole16, shape((1, nb), F32)), 10, 1, ext
    )(near, it, low, high, load, lam, diag, off, prec, stiff_deriv, resp)
    gradient = lax.psum(grad.reshape(nb), "freq")
    return (adjoint[None], gradient)


def solution(mesh):
    in_specs = (
        P("freq", "sub", None, None),
        P("freq", "sub", None),
        P("sub"),
        P("sub"),
        P("freq", "sub", None, None, None),
        P("freq", "sub", None, None, None, None),
        P("sub", None),
        P("freq", "sub", None, None, None),
        P("sub", None, None),
    )
    out_specs = (P("freq", "sub", None, None), P("sub"))
    return jax.shard_map(shards, mesh=mesh, in_specs=in_specs, out_specs=out_specs, check_vma=False)
```

time: 481 us -> 93.8 us (0.20)
  the two profiles are of different devices: /device:TPU:32 before, /device:TPU:8 now
where the time goes in v1:
time: 93.8 us; the launch traced here: 93.4 us
  blocking collectives  43 us (46%)
  Pallas kernels  24.3 us (26%)
  starting transfers between devices  15.4 us (16%)
  local copies, waits for them, and re-layouts  6.7 us (7%)
  waiting for transfers between devices  3.25 us (3%)
    all_to_all x1, blocking collectives, shards(): lax.all_to_all(packed.reshape(peers, SLOTS, cols), 'sub', 0, 0, tiled=True)  32.1 us
    ppermute x2, starting transfers between devices, halo(): lax.ppermute(first, axis, backward)  11.5 us
    psum x1, blocking collectives, shards(): gradient = lax.psum(grad.reshape(nb), 'freq')  11 us
    pallas_call x1, Pallas kernels, shards(): call(functools.partial(last_kernel, scale), (whole16, shape((1, nb), F32)...  10.4 us
    pallas_call x1, Pallas kernels, shards(): call(sweep_kernel, (whole32, whole16, edge, edge), 8, 1, ext)  7.99 us
    unnamed x25, local copies, waits for them, and re-layouts  6.48 us
    pallas_call x1, Pallas kernels, shards(): call(load_kernel, (whole32, whole32, whole16, edge, edge), 3, 0, [pltpu.V...  5.38 us
    ppermute x2, starting transfers between devices, halo(): lax.ppermute(last, axis, forward)  3.83 us
  transfers between devices with their start and end apart: 4, of which 2 were waited for; matrix products, arithmetic and copies ran while one was open for 0% of the time, Pallas kernels for 0%

profile of v1, /device:TPU:8, one launch (start us, length us, event | category | flops | bytes accessed | tf_op | source)
XLA Modules:
  0.0 93.4 jit_solution(12553880759918980282)
XLA Ops:
  0.7 0.9 copy-done.8
  1.5 0.7 copy-done.9
  2.2 0.7 copy-done.10
  2.9 0.4 shard_map.104
  3.3 0.1 reshape.25
  3.4 0.0 copy-start.11
  3.4 32.1 %all_to_all.5 = bf16[128,4,256]{2,1,0:T(4,128)(2,1)S(1)} all-to-all(bf16[128,4,256]{2,1,0:T(4,128)(2,1)S(1)} %reshape.25), channel_id=1, replica_groups=mesh['sub'=128,'freq'=4] {'sub'}, dimensions={0} | all-to-all | bytes 524288 | tf_op jit(solution)/shard_map/all_to_all | solution.py:199
  35.5 0.1 reshape.26.recv_ref
  35.6 5.4 %shard_map.105 = (f32[12,96,256]{2,1,0:T(8,128)S(1)}, f32[12,96,256]{2,1,0:T(8,128)S(1)}, bf16[12,96,256]{2,1,0:T(8,128)(2,1)S(1)}, bf16[96,256]{1,0:T(8,128)(2,1)S(1)}, bf16[96,256]{1,0:T(8,128)(2,1)S(1)}) custom-call(bf16[512,256]{1,0:T(8,128)(2,1)S(1)} %reshape.26.recv_ref, bf16[12,96,256]{2,1,0:T(8,128)(2,1)S(1)} %bitcast.14, ...), custom_call_target="tpu_custom_call" | custom-call | tf_op jit(solution)/shard_map/pallas_call | solution.py:203
  40.9 1.0 %copy-done.3 = f32[12,96,256]{2,1,0:T(8,128)} copy-done((f32[12,96,256]{2,1,0:T(8,128)}, f32[12,96,256]{2,1,0:T(8,128)S(1)}, u32[]{:S(2)}) %copy-start.3) | copy-done | bytes 1179672
  42.0 0.8 copy-done.5
  42.8 1.9 %collective-permute-start = (bf16[96,256]{1,0:T(8,128)(2,1)S(1)}, bf16[96,256]{1,0:T(8,128)(2,1)S(1)}, u32[]{:S(2)}, u32[]{:S(2)}) collective-permute-start(bf16[96,256]{1,0:T(8,128)(2,1)S(1)} %get-tuple-element.14), channel_id=1, source_target_pairs={{0,4},{4,8},{8,12},{12,16},{16,20},{20,24},{24,28},{28,32},{32,36}... | collective-permute-start | bytes 147464 | tf_op jit(solution)/shard_map/ppermute | solution.py:184
  44.7 5.8 %collective-permute-start.1 = (bf16[96,256]{1,0:T(8,128)(2,1)S(1)}, bf16[96,256]{1,0:T(8,128)(2,1)S(1)}, u32[]{:S(2)}, u32[]{:S(2)}) collective-permute-start(bf16[96,256]{1,0:T(8,128)(2,1)S(1)} %get-tuple-element.15), channel_id=1, source_target_pairs={{4,0},{8,4},{12,8},{16,12},{20,16},{24,20},{28,24},{32,28},{36,32}... | collective-permute-start | bytes 147464 | tf_op jit(solution)/shard_map/ppermute | solution.py:184
  50.5 0.1 copy.12
  50.6 0.1 reshape.22.cols_ref
  50.7 1.5 %collective-permute-done.1.high_ref = bf16[96,256]{1,0:T(8,128)(2,1)S(1)} collective-permute-done((bf16[96,256]{1,0:T(8,128)(2,1)S(1)}, bf16[96,256]{1,0:T(8,128)(2,1)S(1)}, u32[]{:S(2)}, u32[]{:S(2)}) %collective-permute-start.1) | collective-permute-done | bytes 49184 | tf_op jit(solution)/shard_map/ppermute | solution.py:184
  52.2 1.3 %copy-done.4 = f32[12,96,256]{2,1,0:T(8,128)S(1)} copy-done((f32[12,96,256]{2,1,0:T(8,128)S(1)}, f32[12,96,256]{2,1,0:T(8,128)}, u32[]{:S(2)}) %copy-start.4) | copy-done | bytes 1179672
  53.5 1.1 %copy-done.6 = bf16[12,96,256]{2,1,0:T(8,128)(2,1)S(1)} copy-done((bf16[12,96,256]{2,1,0:T(8,128)(2,1)S(1)}, bf16[12,96,256]{2,1,0:T(8,128)(2,1)}, u32[]{:S(2)}) %copy-start.6) | copy-done | bytes 589848
  54.5 8.0 %shard_map.106 = (f32[12,96,256]{2,1,0:T(8,128)S(1)}, bf16[12,96,256]{2,1,0:T(8,128)(2,1)S(1)}, bf16[96,256]{1,0:T(8,128)(2,1)S(1)}, bf16[96,256]{1,0:T(8,128)(2,1)S(1)}) custom-call(s32[60]{0:T(128)S(1)} %reshape.22.cols_ref, bf16[12,96,256]{2,1,0:T(8,128)(2,1)S(1)} %copy-done.6, bf16[96,256]{1,0:T(8,128)(2,1)S(1)} %collective-permute-done.low_ref, ...), custom_call_target="tpu_custom_call" | custom-call | tf_op jit(solution)/shard_map/pallas_call | solution.py:212
  62.5 1.9 %collective-permute-start.2 = (bf16[96,256]{1,0:T(8,128)(2,1)S(1)}, bf16[96,256]{1,0:T(8,128)(2,1)S(1)}, u32[]{:S(2)}, u32[]{:S(2)}) collective-permute-start(bf16[96,256]{1,0:T(8,128)(2,1)S(1)} %get-tuple-element.19), channel_id=1, source_target_pairs={{0,4},{4,8},{8,12},{12,16},{16,20},{20,24},{24,28},{28,32},{32,36}... | collective-permute-start | bytes 147464 | tf_op jit(solution)/shard_map/ppermute | solution.py:184
  64.5 5.8 %collective-permute-start.3 = (bf16[96,256]{1,0:T(8,128)(2,1)S(1)}, bf16[96,256]{1,0:T(8,128)(2,1)S(1)}, u32[]{:S(2)}, u32[]{:S(2)}) collective-permute-start(bf16[96,256]{1,0:T(8,128)(2,1)S(1)} %get-tuple-element.20), channel_id=1, source_target_pairs={{4,0},{8,4},{12,8},{16,12},{20,16},{24,20},{28,24},{32,28},{36,32}... | collective-permute-start | bytes 147464 | tf_op jit(solution)/shard_map/ppermute | solution.py:184
  70.3 1.7 %collective-permute-done.3.high_ref = bf16[96,256]{1,0:T(8,128)(2,1)S(1)} collective-permute-done((bf16[96,256]{1,0:T(8,128)(2,1)S(1)}, bf16[96,256]{1,0:T(8,128)(2,1)S(1)}, u32[]{:S(2)}, u32[]{:S(2)}) %collective-permute-start.3) | collective-permute-done | bytes 49184 | tf_op jit(solution)/shard_map/ppermute | solution.py:184
  72.0 10.4 %shard_map.107 = (bf16[12,96,256]{2,1,0:T(8,128)(2,1)}, f32[1,12]{1,0:T(1,128)S(1)}) custom-call(s32[60]{0:T(128)S(1)} %reshape.22.cols_ref, bf16[12,96,256]{2,1,0:T(8,128)(2,1)S(1)} %get-tuple-element.18.it_ref, bf16[96,256]{1,0:T(8,128)(2,1)S(1)} %collective-permute-done.2.low_ref, bf16[96,256]{1,0:T(8,128)(2,1)S(1)} %collective-permute-done.3.high_ref, ...), custom_call_target="tpu_custom_call" | custom-call | tf_op jit(solution)/shard_map/pallas_call | solution.py:217
  82.4 11.0 %psum.7 = f32[12]{0:T(128)} all-reduce(f32[12]{0:T(128)S(1)} %bitcast.19), channel_id=1, replica_groups=mesh['sub'=128,'freq'=4] {'freq'}, use_global_device_ids=true, to_apply=%region_0.0 | all-reduce | flops 12 | bytes 96 | tf_op jit(solution)/shard_map/psum | solution.py:220
  (18 shorter events, 0.0 us)
Async XLA Ops:
  0.6 34.9 %copy-start = (bf16[1,12,2,96,96]{4,3,2,1,0:T(8,128)(2,1)S(1)}, bf16[1,12,2,96,96]{4,3,2,1,0:T(8,128)(2,1)}, u32[]{:S(2)}) copy-start(bf16[1,12,2,96,96]{4,3,2,1,0:T(8,128)(2,1)} %param.16) | copy-start | bytes 1327108
  0.6 34.9 %copy-start.2 = (bf16[1,12,96,256]{3,2,1,0:T(8,128)(2,1)S(1)}, bf16[1,12,96,256]{3,2,1,0:T(8,128)(2,1)}, u32[]{:S(2)}) copy-start(bf16[1,12,96,256]{3,2,1,0:T(8,128)(2,1)} %param.9) | copy-start | bytes 1769476
  0.7 0.9 copy-start.8
  1.5 0.7 copy-start.9
  2.2 0.7 copy-start.10
  3.4 47.1 %copy-start.11 = (s32[12,5]{0,1:T(8,128)S(1)}, s32[12,5]{0,1:T(8,128)}, u32[]{:S(2)}) copy-start(s32[12,5]{0,1:T(8,128)} %param.15) | copy-start | bytes 724
  3.4 48.8 %copy-start.1 = (bf16[1,12,2,96,96]{4,3,2,1,0:T(8,128)(2,1)S(1)}, bf16[1,12,2,96,96]{4,3,2,1,0:T(8,128)(2,1)}, u32[]{:S(2)}) copy-start(bf16[1,12,2,96,96]{4,3,2,1,0:T(8,128)(2,1)} %param.13) | copy-start | bytes 1327108
  40.9 1.0 %copy-start.3 = (f32[12,96,256]{2,1,0:T(8,128)}, f32[12,96,256]{2,1,0:T(8,128)S(1)}, u32[]{:S(2)}) copy-start(f32[12,96,256]{2,1,0:T(8,128)S(1)} %get-tuple-element.17.lam_ref) | copy-start | bytes 3538948
  42.0 0.8 copy-start.5
  42.8 7.9 %collective-permute-start = (bf16[96,256]{1,0:T(8,128)(2,1)S(1)}, bf16[96,256]{1,0:T(8,128)(2,1)S(1)}, u32[]{:S(2)}, u32[]{:S(2)}) collective-permute-start(bf16[96,256]{1,0:T(8,128)(2,1)S(1)} %get-tuple-element.14), channel_id=1, source_target_pairs={{0,4},{4,8},{8,12},{12,16},{16,20},{20,24},{24,28},{28,32},{32,36}... | collective-permute-start | bytes 147464 | tf_op jit(solution)/shard_map/ppermute | solution.py:184
  44.7 7.5 %collective-permute-start.1 = (bf16[96,256]{1,0:T(8,128)(2,1)S(1)}, bf16[96,256]{1,0:T(8,128)(2,1)S(1)}, u32[]{:S(2)}, u32[]{:S(2)}) collective-permute-start(bf16[96,256]{1,0:T(8,128)(2,1)S(1)} %get-tuple-element.15), channel_id=1, source_target_pairs={{4,0},{8,4},{12,8},{16,12},{20,16},{24,20},{28,24},{32,28},{36,32}... | collective-permute-start | bytes 147464 | tf_op jit(solution)/shard_map/ppermute | solution.py:184
  52.2 1.3 %copy-start.4 = (f32[12,96,256]{2,1,0:T(8,128)S(1)}, f32[12,96,256]{2,1,0:T(8,128)}, u32[]{:S(2)}) copy-start(f32[12,96,256]{2,1,0:T(8,128)} %copy-done.3) | copy-start | bytes 3538948
  53.5 1.1 %copy-start.6 = (bf16[12,96,256]{2,1,0:T(8,128)(2,1)S(1)}, bf16[12,96,256]{2,1,0:T(8,128)(2,1)}, u32[]{:S(2)}) copy-start(bf16[12,96,256]{2,1,0:T(8,128)(2,1)} %copy-done.5) | copy-start | bytes 1769476
  54.5 17.5 %copy-start.7 = (bf16[12,96,96]{2,1,0:T(8,128)(2,1)S(1)}, bf16[12,96,96]{2,1,0:T(8,128)(2,1)}, u32[]{:S(2)}) copy-start(bf16[12,96,96]{2,1,0:T(8,128)(2,1)} %stiff_ref.1) | copy-start | bytes 663556
  62.5 7.7 %collective-permute-start.2 = (bf16[96,256]{1,0:T(8,128)(2,1)S(1)}, bf16[96,256]{1,0:T(8,128)(2,1)S(1)}, u32[]{:S(2)}, u32[]{:S(2)}) collective-permute-start(bf16[96,256]{1,0:T(8,128)(2,1)S(1)} %get-tuple-element.19), channel_id=1, source_target_pairs={{0,4},{4,8},{8,12},{12,16},{16,20},{20,24},{24,28},{28,32},{32,36}... | collective-permute-start | bytes 147464 | tf_op jit(solution)/shard_map/ppermute | solution.py:184
  64.5 7.5 %collective-permute-start.3 = (bf16[96,256]{1,0:T(8,128)(2,1)S(1)}, bf16[96,256]{1,0:T(8,128)(2,1)S(1)}, u32[]{:S(2)}, u32[]{:S(2)}) collective-permute-start(bf16[96,256]{1,0:T(8,128)(2,1)S(1)} %get-tuple-element.20), channel_id=1, source_target_pairs={{4,0},{8,4},{12,8},{16,12},{20,16},{24,20},{28,24},{32,28},{36,32}... | collective-permute-start | bytes 147464 | tf_op jit(solution)/shard_map/ppermute | solution.py:184

commit v2 on v1

v2 whole, which is shorter than its diff:
```python
import functools
import math

import jax
import jax.numpy as jnp
from jax import lax
from jax.experimental import pallas as pl
from jax.experimental.pallas import tpu as pltpu
from jax.sharding import PartitionSpec as P

SLOTS = 4
VMEM_LIMIT = 16 * 1024 * 1024

F32 = jnp.float32
BF16 = jnp.bfloat16


def iota(shape, dim):
    return lax.broadcasted_iota(jnp.int32, shape, dim)


def split_product(both):
    m, half = both.shape[0] // 2, both.shape[1] // 2
    real_part = both[:m, :half] - both[m:, half:]
    imag_part = both[:m, half:] + both[m:, :half]
    return jnp.concatenate([real_part, imag_part], axis=1)


def stacked(tile_pair):
    return tile_pair.reshape(tile_pair.shape[0] * tile_pair.shape[1], tile_pair.shape[2])


def complex_product(tile_pair, block):
    return split_product(jnp.dot(stacked(tile_pair), block, preferred_element_type=F32))


def pack_kernel(rows_per, code_ref, measured_ref, out_ref):
    count = measured_ref.shape[0]
    slots_all = out_ref.shape[0]
    code = code_ref[...]
    owner = code.astype(jnp.int32) >> 11
    lanes = jnp.broadcast_to(jnp.pad(code, ((0, 0), (0, 128 - count))), (128, 128))
    code_col = jnp.transpose(lanes)[:count, :count].astype(jnp.int32)
    owner_col = code_col >> 11
    row_col = code_col & 2047
    same = jnp.broadcast_to(owner, (count, count)) == owner_col
    sub = iota((count, count), 0)
    lane = iota((count, count), 1)
    rank_row = jnp.sum(jnp.where(same & (sub < lane), 1, 0), axis=0, keepdims=True)
    rank_col = jnp.sum(jnp.where(same & (lane < sub), 1, 0), axis=1, keepdims=True)
    place = iota((slots_all, count), 0)
    here = (place >> 2) == owner
    slot = place & 3
    pick = jnp.where(here & (slot == rank_row), 1.0, 0.0).astype(BF16)
    tell = jnp.where(here & (slot == SLOTS - 1), 1.0, 0.0).astype(BF16)
    width = iota((count, 128), 1)
    row_wide = jnp.broadcast_to(row_col[:, :1], (count, 128))
    block = row_wide // rows_per
    inner = row_wide - block * rows_per
    numbers = jnp.where(width == rank_col, block + 1, 0) + jnp.where(
        width == rank_col + SLOTS, inner, 0
    )
    numbers = numbers.astype(F32).astype(BF16)
    rows = jnp.dot(pick, measured_ref[...], preferred_element_type=F32)
    told = jnp.dot(tell, numbers, preferred_element_type=F32)
    half = rows.shape[-1] // 2
    out_ref[:, :half] = (rows[:, :half] + told).astype(BF16)
    out_ref[:, half:] = rows[:, half:].astype(BF16)


def send_edges(parity, first, last, partner_ref, other_ref):
    even = parity == 0
    partner_ref[...] = jnp.where(even, last, first).astype(BF16)
    other_ref[...] = jnp.where(even, first, last).astype(BF16)


def take_edges(parity, partner_ref, other_ref, ext_ref):
    top = ext_ref.shape[0] - 1
    even = parity == 0
    ext_ref[jnp.where(even, top, 0)] = partner_ref[...]
    ext_ref[jnp.where(even, 0, top)] = other_ref[...]


def make_load(first, count, place_ref, recv, ones, resp_ref):
    m = place_ref.shape[0]
    half = recv.shape[1] // 2
    place = place_ref[...]
    hit = jnp.concatenate(
        [jnp.where(place == (first + i) * m, 1.0, 0.0).astype(BF16) for i in range(count)], axis=0
    )
    summed = jnp.dot(hit, recv, preferred_element_type=F32)
    number = jnp.dot(hit, ones, preferred_element_type=F32)
    loads = []
    for i in range(count):
        rows = slice(i * m, (i + 1) * m)
        resp = resp_ref[first + i].astype(F32)
        loads.append(
            jnp.concatenate([number[rows], number[rows]], axis=1) * resp - summed[rows]
        )
    return loads


def edge_kernel(parity_ref, recv_ref, resp_ref, prec_ref, place_ref, partner_ref, other_ref):
    nb, m, cols = resp_ref.shape
    half = cols // 2
    places = recv_ref.shape[0]
    recv = recv_ref[...]
    turned = jnp.transpose(recv[:, :half].astype(F32)).astype(BF16)
    lane = iota((m, half), 1)
    slot = iota((m, places), 1) & 3
    where_row = jnp.full((m, places), -1.0, F32)
    for s in range(SLOTS - 1):
        weights = jnp.where(lane == s, m, 0) + jnp.where(lane == s + SLOTS, 1, 0)
        told = jnp.dot(weights.astype(F32).astype(BF16), turned, preferred_element_type=F32)
        told = pltpu.roll(told, places + s - (SLOTS - 1), 1)
        where_row = jnp.where(slot == s, told - m, where_row)
    place_ref[...] = where_row.astype(jnp.int32) - iota((m, places), 0)
    ones = jnp.ones((places, half), BF16)
    edges = []
    for b in (0, nb - 1):
        load = make_load(b, 1, place_ref, recv, ones, resp_ref)[0]
        edges.append(complex_product(prec_ref[b], load.astype(BF16)))
    send_edges(parity_ref[0], *edges, partner_ref, other_ref)


def load_kernel(
    place_ref, recv_ref, resp_ref, prec_ref, stiff_ref, load_ref, lam_ref, ext_ref, stiff_out
):
    nb, m, cols = resp_ref.shape
    recv = recv_ref[...]
    ones = jnp.ones((recv.shape[0], cols // 2), BF16)
    group = 4 if nb % 4 == 0 else 1
    for first in range(0, nb, group):
        loads = make_load(first, group, place_ref, recv, ones, resp_ref)
        for i, load in enumerate(loads):
            b = first + i
            load_ref[b] = load
            lam = complex_product(prec_ref[b], load.astype(BF16))
            lam_ref[b] = lam
            ext_ref[b + 1] = lam.astype(BF16)
    for b in range(nb):
        stiff_out[b] = jnp.dot(stiff_ref[b], resp_ref[b], preferred_element_type=F32)


def sweep_blocks(blocks, cols_ref, ext_ref, load_ref, lam_ref, diag_ref, off_ref, prec_ref):
    near = off_ref.shape[1]
    updates = []
    for b in blocks:
        tiles = [stacked(diag_ref[b])] + [stacked(off_ref[b, k]) for k in range(near)]
        parts = [ext_ref[b + 1]] + [ext_ref[cols_ref[b * near + k]] for k in range(near)]
        both = None
        for i in range(0, near + 1, 2):
            part = jnp.dot(
                jnp.concatenate(tiles[i : i + 2], axis=1),
                jnp.concatenate(parts[i : i + 2], axis=0),
                preferred_element_type=F32,
            )
            both = part if both is None else both + part
        updates.append((load_ref[b] - split_product(both)).astype(BF16))
    for b, update in zip(blocks, updates):
        yield b, lam_ref[b] + complex_product(prec_ref[b], update)


def sweep_edge_kernel(
    parity_ref, cols_ref, from_partner, from_other, load_ref, lam_ref, diag_ref, off_ref, prec_ref,
    _, ext_ref, partner_ref, other_ref,
):
    nb = load_ref.shape[0]
    take_edges(parity_ref[0], from_partner, from_other, ext_ref)
    tiles = (diag_ref, off_ref, prec_ref)
    edges = [lam for _, lam in sweep_blocks((0, nb - 1), cols_ref, ext_ref, load_ref, lam_ref, *tiles)]
    send_edges(parity_ref[0], *edges, partner_ref, other_ref)


def sweep_kernel(
    cols_ref, ext_ref, load_ref, lam_ref, diag_ref, off_ref, prec_ref, lam_out, ext_out
):
    blocks, tiles = range(load_ref.shape[0]), (diag_ref, off_ref, prec_ref)
    for b, lam in sweep_blocks(blocks, cols_ref, ext_ref, load_ref, lam_ref, *tiles):
        lam_out[b] = lam
        ext_out[b + 1] = lam.astype(BF16)


def last_kernel(
    scale, parity_ref, cols_ref, from_partner, from_other, load_ref, lam_ref, diag_ref, off_ref,
    prec_ref, stiff_ref, _, adj_out, grad_out, ext_ref, adj_ref, part_ref, sems,
):
    nb, m, cols = load_ref.shape
    half = cols // 2
    take_edges(parity_ref[0], from_partner, from_other, ext_ref)
    part_ref[...] = jnp.zeros_like(part_ref)
    copies = []
    tiles = (diag_ref, off_ref, prec_ref)
    for b, lam in sweep_blocks(range(nb), cols_ref, ext_ref, load_ref, lam_ref, *tiles):
        adj_ref[b] = lam.astype(BF16)
        copies.append(pltpu.make_async_copy(adj_ref.at[b], adj_out.at[b], sems.at[b]))
        copies[-1].start()
        terms = lam * stiff_ref[b]
        part_ref[b : b + 1] = jnp.sum(terms[:, :half] + terms[:, half:], axis=0, keepdims=True)
    total = jnp.sum(jnp.transpose(part_ref[...]), axis=0, keepdims=True)
    grad_out[...] = total[:, :nb] * scale
    for copy in copies:
        copy.wait()


IN_VMEM = pl.BlockSpec(memory_space=pltpu.VMEM)
IN_SMEM = pl.BlockSpec(memory_space=pltpu.SMEM)
IN_HBM = pl.BlockSpec(memory_space=pltpu.HBM)


def call(kernel, outs, ins, out_specs=None, scratch=(), aliases=None, mflops=1):
    return pl.pallas_call(
        kernel,
        out_shape=outs,
        in_specs=ins,
        out_specs=out_specs or tuple([IN_VMEM] * len(outs)),
        scratch_shapes=list(scratch),
        input_output_aliases=aliases or {},
        compiler_params=pltpu.CompilerParams(vmem_limit_bytes=VMEM_LIMIT),
        cost_estimate=pl.CostEstimate(
            flops=mflops * 1000000, bytes_accessed=4000000, transcendentals=0
        ),
    )


def swap_edges(to_partner, to_other, axis):
    count = lax.axis_size(axis)
    pairs = [(i, i ^ 1) for i in range(count)]
    others = [(i, i - 1 if i % 2 == 0 else i + 1) for i in range(1, count - 1)]
    return lax.ppermute(to_partner, axis, pairs), lax.ppermute(to_other, axis, others)


def shards(
    response, measured, sensor_owner, sensor_row, adj_diag, adj_off, block_cols, precond, stiff_deriv
):
    resp = response[0]
    diag, off, prec = adj_diag[0], adj_off[0], precond[0]
    nb, m, cols = resp.shape
    peers = lax.axis_size("sub")
    sensors = sensor_owner.shape[0]
    shape = jax.ShapeDtypeStruct
    code = (sensor_owner * 2048 + sensor_row).astype(F32).reshape(1, sensors)
    place_id = lax.axis_index("sub") & 1
    near = block_cols.reshape(-1)
    code, place_id, near = lax.optimization_barrier((code, place_id, near))
    (packed,) = call(
        functools.partial(pack_kernel, m), (shape((peers * SLOTS, cols), BF16),), [IN_VMEM] * 2
    )(code, measured[0])
    recv = lax.all_to_all(packed.reshape(peers, SLOTS, cols), "sub", 0, 0, tiled=True)
    recv = recv.reshape(peers * SLOTS, cols)
    parity = place_id.astype(jnp.int32).reshape(1)

    whole32, whole16 = shape((nb, m, cols), F32), shape((nb, m, cols), BF16)
    wide16, edge = shape((nb + 2, m, cols), BF16), shape((m, cols), BF16)
    place, to_partner, to_other = call(
        edge_kernel,
        (shape((m, peers * SLOTS), jnp.int32), edge, edge),
        [IN_SMEM] + [IN_VMEM] * 3,
    )(parity, recv, resp, prec)
    from_partner, from_other = swap_edges(to_partner, to_other, "sub")
    load, lam, ext, stiff_resp = call(
        load_kernel, (whole32, whole32, wide16, whole32), [IN_VMEM] * 5, mflops=2000
    )(place, recv, resp, prec, stiff_deriv)

    ext, to_partner, to_other = call(
        sweep_edge_kernel,
        (wide16, edge, edge),
        [IN_SMEM] * 2 + [IN_VMEM] * 8,
        aliases={9: 0},
    )(parity, near, from_partner, from_other, load, lam, diag, off, prec, ext)
    from_partner, from_other = swap_edges(to_partner, to_other, "sub")
    lam, ext = call(sweep_kernel, (whole32, wide16), [IN_SMEM] + [IN_VMEM] * 6, mflops=2000)(
        near, ext, load, lam, diag, off, prec
    )

    scale = 1.0 / math.sqrt(m * cols)
    adjoint, grad, _ = call(
        functools.partial(last_kernel, scale),
        (whole16, shape((1, nb), F32), wide16),
        [IN_SMEM] * 2 + [IN_VMEM] * 9,
        out_specs=(IN_HBM, IN_VMEM, IN_VMEM),
        scratch=[
            pltpu.VMEM((nb, m, cols), BF16),
            pltpu.VMEM((128, 128), F32),
            pltpu.SemaphoreType.DMA((nb,)),
        ],
        aliases={10: 2},
    )(parity, near, from_partner, from_other, load, lam, diag, off, prec, stiff_resp, ext)
    gradient = lax.psum(grad.reshape(nb), "freq")
    return (adjoint[None], gradient)


def solution(mesh):
    in_specs = (
        P("freq", "sub", None, None),
        P("freq", "sub", None),
        P("sub"),
        P("sub"),
        P("freq", "sub", None, None, None),
        P("freq", "sub", None, None, None, None),
        P("sub", None),
        P("freq", "sub", None, None, None),
        P("sub", None, None),
    )
    out_specs = (P("freq", "sub", None, None), P("sub"))
    return jax.shard_map(shards, mesh=mesh, in_specs=in_specs, out_specs=out_specs, check_vma=False)
```

time: 93.8 us -> 71 us (0.76)
  Pallas kernels: 24.3 us -> 8.97 us
  starting transfers between devices: 15.4 us -> 8.46 us
  local copies, waits for them, and re-layouts: 6.7 us -> 1.91 us
  waiting for transfers between devices: 3.25 us -> 6.77 us
    pallas_call x3 -> x5, Pallas kernels: 13.8 us -> 6.11 us  [the longest x1 2.07 us: shards(): call(sweep_kernel, (whole32, wide16), [IN_SMEM] + [IN_VMEM] * 6, mflops=2...]
    pallas_call x1, Pallas kernels: 10.4 us -> 2.86 us  [shards(): call(functools.partial(last_kernel, scale), (whole16, shape((1, nb), F32)...]
    ppermute x4, starting transfers between devices: 15.4 us -> 8.46 us  [the longest x2 4.62 us: swap_edges(): lax.ppermute(to_other, axis, others)]
    unnamed x25 -> x13, local copies, waits for them, and re-layouts: 6.48 us -> 1.69 us
    ppermute x4, waiting for transfers between devices: 3.25 us -> 6.77 us  [the longest x2 6.77 us: swap_edges(): lax.ppermute(to_other, axis, others)]
  transfers between devices with their start and end apart: 4 -> 4, of which waited for: 2 -> 2; matrix products, arithmetic and copies ran while one was open for 0% -> 0% of each run, Pallas kernels for 0% -> 5%
where the time goes in v2:
time: 71 us; the launch traced here: 70.7 us
  blocking collectives  43.1 us (61%)
  Pallas kernels  8.97 us (13%)
  starting transfers between devices  8.46 us (12%)
  waiting for transfers between devices  6.77 us (10%)
  local copies, waits for them, and re-layouts  1.91 us (3%)
  between operations  0.8 us (1%)
    all_to_all x1, blocking collectives, shards(): lax.all_to_all(packed.reshape(peers, SLOTS, cols), 'sub', 0, 0, tiled=True)  32.1 us
    psum x1, blocking collectives, shards(): gradient = lax.psum(grad.reshape(nb), 'freq')  11 us
    ppermute x2, waiting for transfers between devices, swap_edges(): lax.ppermute(to_other, axis, others)  6.77 us
    ppermute x2, starting transfers between devices, swap_edges(): lax.ppermute(to_other, axis, others)  4.62 us
    ppermute x2, starting transfers between devices, swap_edges(): lax.ppermute(to_partner, axis, pairs)  3.84 us
    pallas_call x1, Pallas kernels, shards(): call(functools.partial(last_kernel, scale), (whole16, shape((1, nb), F32)...  2.86 us
    pallas_call x1, Pallas kernels, shards(): call(sweep_kernel, (whole32, wide16), [IN_SMEM] + [IN_VMEM] * 6, mflops=2...  2.07 us
    unnamed x13, local copies, waits for them, and re-layouts  1.69 us
  transfers between devices with their start and end apart: 4, of which 2 were waited for; matrix products, arithmetic and copies ran while one was open for 0% of the time, Pallas kernels for 5%

profile of v2, /device:TPU:8, one launch (start us, length us, event | category | flops | bytes accessed | tf_op | source)
XLA Modules:
  0.0 70.7 jit_solution(9684358027649004644)
XLA Ops:
  0.7 0.9 %copy.14 = s32[12,5]{1,0:T(8,128)S(1)} copy(s32[12,5]{0,1:T(8,128)} %param.15) | data formatting | bytes 480 | tf_op args[6]
  1.5 0.1 reshape.23.cols_ref
  1.6 0.7 convert_bitcast_fusion.code_ref
  2.3 0.8 %copy-done.4 = bf16[1,96,256]{2,1,0:T(8,128)(2,1)S(1)} copy-done((bf16[1,96,256]{2,1,0:T(8,128)(2,1)S(1)}, bf16[1,96,256]{2,1,0:T(8,128)(2,1)}, u32[]{:S(2)}) %copy-start.4) | copy-done | bytes 49176
  3.1 0.4 shard_map.104
  3.5 0.1 reshape.25
  3.6 0.0 copy-start.5
  3.6 32.1 %all_to_all.5 = bf16[128,4,256]{2,1,0:T(4,128)(2,1)S(1)} all-to-all(bf16[128,4,256]{2,1,0:T(4,128)(2,1)S(1)} %reshape.25), channel_id=1, replica_groups=mesh['sub'=128,'freq'=4] {'sub'}, dimensions={0} | all-to-all | bytes 524288 | tf_op jit(solution)/shard_map/all_to_all | solution.py:249
  35.7 0.1 reshape.26.recv_ref
  35.8 1.0 %shard_map.105 = (s32[96,512]{1,0:T(8,128)S(1)}, bf16[96,256]{1,0:T(8,128)(2,1)S(1)}, bf16[96,256]{1,0:T(8,128)(2,1)S(1)}) custom-call(s32[1]{0:T(128)} %bitcast.1.parity_ref, bf16[512,256]{1,0:T(8,128)(2,1)S(1)} %reshape.26.recv_ref, bf16[12,96,256]{2,1,0:T(8,128)(2,1)S(1)} %bitcast.21, bf16[12,2,96,96]{3,2,1,0:T(8,128)(2,1)S(1)} %bitcast.13), custom_call_target="tpu_custom_call" | custom-call | flops 1000000 | bytes 4000000 | tf_op jit(solution)/shard_map/pallas_call | solution.py:255
  36.8 1.9 %collective-permute-start = (bf16[96,256]{1,0:T(8,128)(2,1)S(1)}, bf16[96,256]{1,0:T(8,128)(2,1)S(1)}, u32[]{:S(2)}, u32[]{:S(2)}) collective-permute-start(bf16[96,256]{1,0:T(8,128)(2,1)S(1)} %get-tuple-element.22), channel_id=1, source_target_pairs={{0,4},{4,0},{8,12},{12,8},{16,20},{20,16},{24,28},{28,24},{32,36},... | collective-permute-start | bytes 147464 | tf_op jit(solution)/shard_map/ppermute | solution.py:230
  38.7 2.3 %collective-permute-start.1 = (bf16[96,256]{1,0:T(8,128)(2,1)S(1)}, bf16[96,256]{1,0:T(8,128)(2,1)S(1)}, u32[]{:S(2)}, u32[]{:S(2)}) collective-permute-start(bf16[96,256]{1,0:T(8,128)(2,1)S(1)} %get-tuple-element.23), channel_id=1, source_target_pairs={{4,8},{8,4},{12,16},{16,12},{20,24},{24,20},{28,32},{32,28},{36,40... | collective-permute-start | bytes 147464 | tf_op jit(solution)/shard_map/ppermute | solution.py:230
  41.1 0.0 copy-start
  41.1 0.0 copy-start.2
  41.1 1.5 %shard_map.106 = (f32[12,96,256]{2,1,0:T(8,128)S(1)}, f32[12,96,256]{2,1,0:T(8,128)S(1)}, bf16[14,96,256]{2,1,0:T(8,128)(2,1)S(1)}, f32[12,96,256]{2,1,0:T(8,128)S(1)}) custom-call(s32[96,512]{1,0:T(8,128)S(1)} %get-tuple-element.24.place_ref, bf16[512,256]{1,0:T(8,128)(2,1)S(1)} %reshape.26.recv_ref, bf16[12,96,256]{2,1,0:T(8,128)(2,1)S(1)} %bitcast.22, ...), custom_call_target="tpu_custom_call" | custom-call | flops 2000000000 | bytes 4000000 | tf_op jit(solution)/shard_map/pallas_call | solution.py:261
  42.6 0.0 collective-permute-done.from_partner
  42.6 3.7 %collective-permute-done.1.from_other = bf16[96,256]{1,0:T(8,128)(2,1)S(1)} collective-permute-done((bf16[96,256]{1,0:T(8,128)(2,1)S(1)}, bf16[96,256]{1,0:T(8,128)(2,1)S(1)}, u32[]{:S(2)}, u32[]{:S(2)}) %collective-permute-start.1) | collective-permute-done | bytes 49184 | tf_op jit(solution)/shard_map/ppermute | solution.py:230
  46.2 1.1 %shard_map.107 = (bf16[14,96,256]{2,1,0:T(8,128)(2,1)S(1)}, bf16[96,256]{1,0:T(8,128)(2,1)S(1)}, bf16[96,256]{1,0:T(8,128)(2,1)S(1)}) custom-call(s32[1]{0:T(128)} %bitcast.1.parity_ref, s32[60]{0:T(128)S(1)} %reshape.23.cols_ref, bf16[96,256]{1,0:T(8,128)(2,1)S(1)} %collective-permute-done.from_partner, ...), custom_call_target="tpu_custom_call", output_to_operand_aliasing={{0}: (9, {})} | custom-call | flops 1000000 | bytes 4000000 | tf_op jit(solution)/shard_map/pallas_call | solution.py:265
  47.3 1.9 %collective-permute-start.2 = (bf16[96,256]{1,0:T(8,128)(2,1)S(1)}, bf16[96,256]{1,0:T(8,128)(2,1)S(1)}, u32[]{:S(2)}, u32[]{:S(2)}) collective-permute-start(bf16[96,256]{1,0:T(8,128)(2,1)S(1)} %get-tuple-element.28), channel_id=1, source_target_pairs={{0,4},{4,0},{8,12},{12,8},{16,20},{20,16},{24,28},{28,24},{32,36},... | collective-permute-start | bytes 147464 | tf_op jit(solution)/shard_map/ppermute | solution.py:230
  49.3 2.3 %collective-permute-start.3 = (bf16[96,256]{1,0:T(8,128)(2,1)S(1)}, bf16[96,256]{1,0:T(8,128)(2,1)S(1)}, u32[]{:S(2)}, u32[]{:S(2)}) collective-permute-start(bf16[96,256]{1,0:T(8,128)(2,1)S(1)} %get-tuple-element.29), channel_id=1, source_target_pairs={{4,8},{8,4},{12,16},{16,12},{20,24},{24,20},{28,32},{32,28},{36,40... | collective-permute-start | bytes 147464 | tf_op jit(solution)/shard_map/ppermute | solution.py:230
  51.6 2.1 %shard_map.108 = (f32[12,96,256]{2,1,0:T(8,128)S(1)}, bf16[14,96,256]{2,1,0:T(8,128)(2,1)S(1)}) custom-call(s32[60]{0:T(128)S(1)} %reshape.23.cols_ref, bf16[14,96,256]{2,1,0:T(8,128)(2,1)S(1)} %get-tuple-element.30.ext_ref, f32[12,96,256]{2,1,0:T(8,128)S(1)} %get-tuple-element.25.load_ref, f32[12,96,256]{2,1,0:T(8,128)S(1)} %get-tuple-element.26.lam_ref, ...), custom_call_target="tpu_custom_call" | custom-call | flops 2000000000 | bytes 4000000 | tf_op jit(solution)/shard_map/pallas_call | solution.py:272
  53.7 3.1 %collective-permute-done.3.from_other = bf16[96,256]{1,0:T(8,128)(2,1)S(1)} collective-permute-done((bf16[96,256]{1,0:T(8,128)(2,1)S(1)}, bf16[96,256]{1,0:T(8,128)(2,1)S(1)}, u32[]{:S(2)}, u32[]{:S(2)}) %collective-permute-start.3) | collective-permute-done | bytes 49184 | tf_op jit(solution)/shard_map/ppermute | solution.py:230
  56.8 2.9 %shard_map.109 = (bf16[12,96,256]{2,1,0:T(8,128)(2,1)}, f32[1,12]{1,0:T(1,128)S(1)}, bf16[14,96,256]{2,1,0:T(8,128)(2,1)S(1)}) custom-call(s32[1]{0:T(128)} %bitcast.1.parity_ref, s32[60]{0:T(128)S(1)} %reshape.23.cols_ref, bf16[96,256]{1,0:T(8,128)(2,1)S(1)} %collective-permute-done.2.from_partner, ...), custom_call_target="tpu_custom_call", output_to_operand_aliasing={{2}: (10, {})} | custom-call | flops 1000000 | bytes 4000000 | tf_op jit(solution)/shard_map/pallas_call | solution.py:277
  59.7 11.0 %psum.7 = f32[12]{0:T(128)} all-reduce(f32[12]{0:T(128)S(1)} %bitcast.24), channel_id=1, replica_groups=mesh['sub'=128,'freq'=4] {'freq'}, use_global_device_ids=true, to_apply=%region_0.0 | all-reduce | flops 12 | bytes 96 | tf_op jit(solution)/shard_map/psum | solution.py:289
  (9 shorter events, 0.0 us)
Async XLA Ops:
  0.6 35.1 %copy-start.1 = (bf16[1,12,2,96,96]{4,3,2,1,0:T(8,128)(2,1)S(1)}, bf16[1,12,2,96,96]{4,3,2,1,0:T(8,128)(2,1)}, u32[]{:S(2)}) copy-start(bf16[1,12,2,96,96]{4,3,2,1,0:T(8,128)(2,1)} %param.16) | copy-start | bytes 1327108
  0.6 35.1 %copy-start.3 = (bf16[1,12,96,256]{3,2,1,0:T(8,128)(2,1)S(1)}, bf16[1,12,96,256]{3,2,1,0:T(8,128)(2,1)}, u32[]{:S(2)}) copy-start(bf16[1,12,96,256]{3,2,1,0:T(8,128)(2,1)} %param.9) | copy-start | bytes 1769476
  2.3 0.8 %copy-start.4 = (bf16[1,96,256]{2,1,0:T(8,128)(2,1)S(1)}, bf16[1,96,256]{2,1,0:T(8,128)(2,1)}, u32[]{:S(2)}) copy-start(bf16[1,96,256]{2,1,0:T(8,128)(2,1)} %param.10) | copy-start | bytes 147460
  3.6 37.4 %copy-start.5 = (bf16[12,96,96]{2,1,0:T(8,128)(2,1)S(1)}, bf16[12,96,96]{2,1,0:T(8,128)(2,1)}, u32[]{:S(2)}) copy-start(bf16[12,96,96]{2,1,0:T(8,128)(2,1)} %stiff_ref.1) | copy-start | bytes 663556
  36.8 5.8 %collective-permute-start = (bf16[96,256]{1,0:T(8,128)(2,1)S(1)}, bf16[96,256]{1,0:T(8,128)(2,1)S(1)}, u32[]{:S(2)}, u32[]{:S(2)}) collective-permute-start(bf16[96,256]{1,0:T(8,128)(2,1)S(1)} %get-tuple-element.22), channel_id=1, source_target_pairs={{0,4},{4,0},{8,12},{12,8},{16,20},{20,16},{24,28},{28,24},{32,36},... | collective-permute-start | bytes 147464 | tf_op jit(solution)/shard_map/ppermute | solution.py:230
  38.7 7.5 %collective-permute-start.1 = (bf16[96,256]{1,0:T(8,128)(2,1)S(1)}, bf16[96,256]{1,0:T(8,128)(2,1)S(1)}, u32[]{:S(2)}, u32[]{:S(2)}) collective-permute-start(bf16[96,256]{1,0:T(8,128)(2,1)S(1)} %get-tuple-element.23), channel_id=1, source_target_pairs={{4,8},{8,4},{12,16},{16,12},{20,24},{24,20},{28,32},{32,28},{36,40... | collective-permute-start | bytes 147464 | tf_op jit(solution)/shard_map/ppermute | solution.py:230
  41.1 5.2 %copy-start = (bf16[1,12,5,2,96,96]{5,4,3,2,1,0:T(8,128)(2,1)S(1)}, bf16[1,12,5,2,96,96]{5,4,3,2,1,0:T(8,128)(2,1)}, u32[]{:S(2)}) copy-start(bf16[1,12,5,2,96,96]{5,4,3,2,1,0:T(8,128)(2,1)} %param.14) | copy-start | bytes 6635524
  41.1 5.2 %copy-start.2 = (bf16[1,12,2,96,96]{4,3,2,1,0:T(8,128)(2,1)S(1)}, bf16[1,12,2,96,96]{4,3,2,1,0:T(8,128)(2,1)}, u32[]{:S(2)}) copy-start(bf16[1,12,2,96,96]{4,3,2,1,0:T(8,128)(2,1)} %param.13) | copy-start | bytes 1327108
  47.3 6.3 %collective-permute-start.2 = (bf16[96,256]{1,0:T(8,128)(2,1)S(1)}, bf16[96,256]{1,0:T(8,128)(2,1)S(1)}, u32[]{:S(2)}, u32[]{:S(2)}) collective-permute-start(bf16[96,256]{1,0:T(8,128)(2,1)S(1)} %get-tuple-element.28), channel_id=1, source_target_pairs={{0,4},{4,0},{8,12},{12,8},{16,20},{20,16},{24,28},{28,24},{32,36},... | collective-permute-start | bytes 147464 | tf_op jit(solution)/shard_map/ppermute | solution.py:230
  49.3 7.5 %collective-permute-start.3 = (bf16[96,256]{1,0:T(8,128)(2,1)S(1)}, bf16[96,256]{1,0:T(8,128)(2,1)S(1)}, u32[]{:S(2)}, u32[]{:S(2)}) collective-permute-start(bf16[96,256]{1,0:T(8,128)(2,1)S(1)} %get-tuple-element.29), channel_id=1, source_target_pairs={{4,8},{8,4},{12,16},{16,12},{20,24},{24,20},{28,32},{32,28},{36,40... | collective-permute-start | bytes 147464 | tf_op jit(solution)/shard_map/ppermute | solution.py:230

commit v3 on v2

--- a/solution.py
+++ b/solution.py
@@ -68,13 +68,13 @@
     out_ref[:, half:] = rows[:, half:].astype(BF16)
 
 
-def send_edges(parity, first, last, partner_ref, other_ref):
+def send_edges(parity, first, last, other_ref, partner_ref):
     even = parity == 0
     partner_ref[...] = jnp.where(even, last, first).astype(BF16)
     other_ref[...] = jnp.where(even, first, last).astype(BF16)
 
 
-def take_edges(parity, partner_ref, other_ref, ext_ref):
+def take_edges(parity, other_ref, partner_ref, ext_ref):
     top = ext_ref.shape[0] - 1
     even = parity == 0
     ext_ref[jnp.where(even, top, 0)] = partner_ref[...]
@@ -100,7 +100,7 @@
     return loads
 
 
-def edge_kernel(parity_ref, recv_ref, resp_ref, prec_ref, place_ref, partner_ref, other_ref):
+def edge_kernel(parity_ref, recv_ref, resp_ref, prec_ref, place_ref, other_ref, partner_ref):
     nb, m, cols = resp_ref.shape
     half = cols // 2
     places = recv_ref.shape[0]
@@ -120,7 +120,7 @@
     for b in (0, nb - 1):
         load = make_load(b, 1, place_ref, recv, ones, resp_ref)[0]
         edges.append(complex_product(prec_ref[b], load.astype(BF16)))
-    send_edges(parity_ref[0], *edges, partner_ref, other_ref)
+    send_edges(parity_ref[0], *edges, other_ref, partner_ref)
 
 
 def load_kernel(
@@ -147,7 +147,7 @@
     updates = []
     for b in blocks:
         tiles = [stacked(diag_ref[b])] + [stacked(off_ref[b, k]) for k in range(near)]
-        parts = [ext_ref[b + 1]] + [ext_ref[cols_ref[b * near + k]] for k in range(near)]
+        parts = [ext_ref[b + 1]] + [ext_ref[cols_ref[k, b]] for k in range(near)]
         both = None
         for i in range(0, near + 1, 2):
             part = jnp.dot(
@@ -162,14 +162,14 @@
 
 
 def sweep_edge_kernel(
-    parity_ref, cols_ref, from_partner, from_other, load_ref, lam_ref, diag_ref, off_ref, prec_ref,
-    _, ext_ref, partner_ref, other_ref,
+    parity_ref, cols_ref, from_other, from_partner, load_ref, lam_ref, diag_ref, off_ref, prec_ref,
+    _, ext_ref, other_ref, partner_ref,
 ):
     nb = load_ref.shape[0]
-    take_edges(parity_ref[0], from_partner, from_other, ext_ref)
+    take_edges(parity_ref[0], from_other, from_partner, ext_ref)
     tiles = (diag_ref, off_ref, prec_ref)
     edges = [lam for _, lam in sweep_blocks((0, nb - 1), cols_ref, ext_ref, load_ref, lam_ref, *tiles)]
-    send_edges(parity_ref[0], *edges, partner_ref, other_ref)
+    send_edges(parity_ref[0], *edges, other_ref, partner_ref)
 
 
 def sweep_kernel(
@@ -182,12 +182,12 @@
 
 
 def last_kernel(
-    scale, parity_ref, cols_ref, from_partner, from_other, load_ref, lam_ref, diag_ref, off_ref,
+    scale, parity_ref, cols_ref, from_other, from_partner, load_ref, lam_ref, diag_ref, off_ref,
     prec_ref, stiff_ref, _, adj_out, grad_out, ext_ref, adj_ref, part_ref, sems,
 ):
     nb, m, cols = load_ref.shape
     half = cols // 2
-    take_edges(parity_ref[0], from_partner, from_other, ext_ref)
+    take_edges(parity_ref[0], from_other, from_partner, ext_ref)
     part_ref[...] = jnp.zeros_like(part_ref)
     copies = []
     tiles = (diag_ref, off_ref, prec_ref)
@@ -223,11 +223,11 @@
     )
 
 
-def swap_edges(to_partner, to_other, axis):
+def swap_edges(to_other, to_partner, axis):
     count = lax.axis_size(axis)
     pairs = [(i, i ^ 1) for i in range(count)]
     others = [(i, i - 1 if i % 2 == 0 else i + 1) for i in range(1, count - 1)]
-    return lax.ppermute(to_partner, axis, pairs), lax.ppermute(to_other, axis, others)
+    return lax.ppermute(to_other, axis, others), lax.ppermute(to_partner, axis, pairs)
 
 
 def shards(
@@ -241,8 +241,8 @@
     shape = jax.ShapeDtypeStruct
     code = (sensor_owner * 2048 + sensor_row).astype(F32).reshape(1, sensors)
     place_id = lax.axis_index("sub") & 1
-    near = block_cols.reshape(-1)
-    code, place_id, near = lax.optimization_barrier((code, place_id, near))
+    near = block_cols.T
+    code, place_id = lax.optimization_barrier((code, place_id))
     (packed,) = call(
         functools.partial(pack_kernel, m), (shape((peers * SLOTS, cols), BF16),), [IN_VMEM] * 2
     )(code, measured[0])
@@ -252,23 +252,23 @@
 
     whole32, whole16 = shape((nb, m, cols), F32), shape((nb, m, cols), BF16)
     wide16, edge = shape((nb + 2, m, cols), BF16), shape((m, cols), BF16)
-    place, to_partner, to_other = call(
+    place, to_other, to_partner = call(
         edge_kernel,
         (shape((m, peers * SLOTS), jnp.int32), edge, edge),
         [IN_SMEM] + [IN_VMEM] * 3,
     )(parity, recv, resp, prec)
-    from_partner, from_other = swap_edges(to_partner, to_other, "sub")
+    from_other, from_partner = swap_edges(to_other, to_partner, "sub")
     load, lam, ext, stiff_resp = call(
         load_kernel, (whole32, whole32, wide16, whole32), [IN_VMEM] * 5, mflops=2000
     )(place, recv, resp, prec, stiff_deriv)
 
-    ext, to_partner, to_other = call(
+    ext, to_other, to_partner = call(
         sweep_edge_kernel,
         (wide16, edge, edge),
         [IN_SMEM] * 2 + [IN_VMEM] * 8,
         aliases={9: 0},
-    )(parity, near, from_partner, from_other, load, lam, diag, off, prec, ext)
-    from_partner, from_other = swap_edges(to_partner, to_other, "sub")
+    )(parity, near, from_other, from_partner, load, lam, diag, off, prec, ext)
+    from_other, from_partner = swap_edges(to_other, to_partner, "sub")
     lam, ext = call(sweep_kernel, (whole32, wide16), [IN_SMEM] + [IN_VMEM] * 6, mflops=2000)(
         near, ext, load, lam, diag, off, prec
     )
@@ -285,7 +285,7 @@
             pltpu.SemaphoreType.DMA((nb,)),
         ],
         aliases={10: 2},
-    )(parity, near, from_partner, from_other, load, lam, diag, off, prec, stiff_resp, ext)
+    )(parity, near, from_other, from_partner, load, lam, diag, off, prec, stiff_resp, ext)
     gradient = lax.psum(grad.reshape(nb), "freq")
     return (adjoint[None], gradient)
 

time: 71 us -> 67 us (0.944)
  waiting for transfers between devices: 6.77 us -> 1.45 us
  starting transfers between devices: 8.46 us -> 10.5 us
  local copies, waits for them, and re-layouts: 1.91 us -> 0.96 us
    ppermute x2, waiting for transfers between devices: 6.77 us -> 1.44 us  [swap_edges(): lax.ppermute(to_other, axis, others)]
    ppermute x2, starting transfers between devices: 4.62 us -> 5.97 us  [swap_edges(): lax.ppermute(to_other, axis, others)]
    unnamed x13 -> x14, local copies, waits for them, and re-layouts: 1.69 us -> 0.83 us
  transfers between devices with their start and end apart: 4 -> 4, of which waited for: 2 -> 1; matrix products, arithmetic and copies ran while one was open for 0% -> 0% of each run, Pallas kernels for 5% -> 5%
where the time goes in v3:
time: 67 us; the launch traced here: 66.7 us
  blocking collectives  43.1 us (64%)
  starting transfers between devices  10.5 us (16%)
  Pallas kernels  9.18 us (14%)
  waiting for transfers between devices  1.45 us (2%)
  local copies, waits for them, and re-layouts  0.96 us (1%)
  between operations  0.82 us (1%)
  other arithmetic  0.77 us (1%)
    all_to_all x1, blocking collectives, shards(): lax.all_to_all(packed.reshape(peers, SLOTS, cols), 'sub', 0, 0, tiled=True)  32.1 us
    psum x1, blocking collectives, shards(): gradient = lax.psum(grad.reshape(nb), 'freq')  11 us
    ppermute x2, starting transfers between devices, swap_edges(): lax.ppermute(to_other, axis, others)  5.97 us
    ppermute x2, starting transfers between devices, swap_edges(): lax.ppermute(to_partner, axis, pairs)  4.51 us
    pallas_call x1, Pallas kernels, shards(): call(functools.partial(last_kernel, scale), (whole16, shape((1, nb), F32)...  2.93 us
    pallas_call x1, Pallas kernels, shards(): call(sweep_kernel, (whole32, wide16), [IN_SMEM] + [IN_VMEM] * 6, mflops=2...  2.14 us
    pallas_call x1, Pallas kernels, shards(): call(load_kernel, (whole32, whole32, wide16, whole32), [IN_VMEM] * 5, mfl...  1.5 us
    ppermute x2, waiting for transfers between devices, swap_edges(): lax.ppermute(to_other, axis, others)  1.44 us
  transfers between devices with their start and end apart: 4, of which 1 were waited for; matrix products, arithmetic and copies ran while one was open for 0% of the time, Pallas kernels for 5%

profile of v3, /device:TPU:8, one launch (start us, length us, event | category | flops | bytes accessed | tf_op | source)
XLA Modules:
  0.0 66.7 jit_solution(2542397444953342203)
XLA Ops:
  0.7 0.8 %convert_bitcast_fusion.code_ref = f32[1,96]{1,0:T(1,128)S(1)} fusion(s32[96]{0:T(128)} %param.12, s32[96]{0:T(128)} %param.11), kind=kLoop, calls=%fused_computation | loop fusion | flops 288 | bytes 1152 | tf_op jit(solution)/shard_map/reshape | solution.py:242
  1.4 0.8 %copy-done.4 = bf16[1,96,256]{2,1,0:T(8,128)(2,1)S(1)} copy-done((bf16[1,96,256]{2,1,0:T(8,128)(2,1)S(1)}, bf16[1,96,256]{2,1,0:T(8,128)(2,1)}, u32[]{:S(2)}) %copy-start.4) | copy-done | bytes 49176
  2.2 0.4 shard_map.104
  2.7 0.1 reshape.21
  2.7 0.0 copy-start.6
  2.8 32.1 %all_to_all.5 = bf16[128,4,256]{2,1,0:T(4,128)(2,1)S(1)} all-to-all(bf16[128,4,256]{2,1,0:T(4,128)(2,1)S(1)} %reshape.21), channel_id=1, replica_groups=mesh['sub'=128,'freq'=4] {'sub'}, dimensions={0} | all-to-all | bytes 524288 | tf_op jit(solution)/shard_map/all_to_all | solution.py:249
  34.8 0.1 reshape.22.recv_ref
  34.9 1.0 %shard_map.105 = (s32[96,512]{1,0:T(8,128)S(1)}, bf16[96,256]{1,0:T(8,128)(2,1)S(1)}, bf16[96,256]{1,0:T(8,128)(2,1)S(1)}) custom-call(s32[1]{0:T(128)} %bitcast.1.parity_ref, bf16[512,256]{1,0:T(8,128)(2,1)S(1)} %reshape.22.recv_ref, bf16[12,96,256]{2,1,0:T(8,128)(2,1)S(1)} %bitcast.22, bf16[12,2,96,96]{3,2,1,0:T(8,128)(2,1)S(1)} %bitcast.14), custom_call_target="tpu_custom_call" | custom-call | flops 1000000 | bytes 4000000 | tf_op jit(solution)/shard_map/pallas_call | solution.py:255
  35.9 1.9 %collective-permute-start = (bf16[96,256]{1,0:T(8,128)(2,1)S(1)}, bf16[96,256]{1,0:T(8,128)(2,1)S(1)}, u32[]{:S(2)}, u32[]{:S(2)}) collective-permute-start(bf16[96,256]{1,0:T(8,128)(2,1)S(1)} %get-tuple-element.20), channel_id=1, source_target_pairs={{4,8},{8,4},{12,16},{16,12},{20,24},{24,20},{28,32},{32,28},{36,40... | collective-permute-start | bytes 147464 | tf_op jit(solution)/shard_map/ppermute | solution.py:230
  37.9 2.6 %collective-permute-start.1 = (bf16[96,256]{1,0:T(8,128)(2,1)S(1)}, bf16[96,256]{1,0:T(8,128)(2,1)S(1)}, u32[]{:S(2)}, u32[]{:S(2)}) collective-permute-start(bf16[96,256]{1,0:T(8,128)(2,1)S(1)} %get-tuple-element.21), channel_id=1, source_target_pairs={{0,4},{4,0},{8,12},{12,8},{16,20},{20,16},{24,28},{28,24},{32,36},... | collective-permute-start | bytes 147464 | tf_op jit(solution)/shard_map/ppermute | solution.py:230
  40.5 0.0 copy-start
  40.5 0.0 copy-start.2
  40.5 0.0 copy-start.5
  40.5 1.5 %shard_map.106 = (f32[12,96,256]{2,1,0:T(8,128)S(1)}, f32[12,96,256]{2,1,0:T(8,128)S(1)}, bf16[14,96,256]{2,1,0:T(8,128)(2,1)S(1)}, f32[12,96,256]{2,1,0:T(8,128)S(1)}) custom-call(s32[96,512]{1,0:T(8,128)S(1)} %get-tuple-element.22.place_ref, bf16[512,256]{1,0:T(8,128)(2,1)S(1)} %reshape.22.recv_ref, bf16[12,96,256]{2,1,0:T(8,128)(2,1)S(1)} %bitcast.23, ...), custom_call_target="tpu_custom_call" | custom-call | flops 2000000000 | bytes 4000000 | tf_op jit(solution)/shard_map/pallas_call | solution.py:261
  42.0 1.4 %collective-permute-done.from_other = bf16[96,256]{1,0:T(8,128)(2,1)S(1)} collective-permute-done((bf16[96,256]{1,0:T(8,128)(2,1)S(1)}, bf16[96,256]{1,0:T(8,128)(2,1)S(1)}, u32[]{:S(2)}, u32[]{:S(2)}) %collective-permute-start) | collective-permute-done | bytes 49184 | tf_op jit(solution)/shard_map/ppermute | solution.py:230
  43.4 0.0 collective-permute-done.1.from_partner
  43.5 1.2 %shard_map.107 = (bf16[14,96,256]{2,1,0:T(8,128)(2,1)S(1)}, bf16[96,256]{1,0:T(8,128)(2,1)S(1)}, bf16[96,256]{1,0:T(8,128)(2,1)S(1)}) custom-call(s32[1]{0:T(128)} %bitcast.1.parity_ref, s32[5,12]{1,0:T(8,128)S(1)} %bitcast.25, bf16[96,256]{1,0:T(8,128)(2,1)S(1)} %collective-permute-done.from_other, ...), custom_call_target="tpu_custom_call", output_to_operand_aliasing={{0}: (9, {})} | custom-call | flops 1000000 | bytes 4000000 | tf_op jit(solution)/shard_map/pallas_call | solution.py:265
  44.6 4.0 %collective-permute-start.2 = (bf16[96,256]{1,0:T(8,128)(2,1)S(1)}, bf16[96,256]{1,0:T(8,128)(2,1)S(1)}, u32[]{:S(2)}, u32[]{:S(2)}) collective-permute-start(bf16[96,256]{1,0:T(8,128)(2,1)S(1)} %get-tuple-element.26), channel_id=1, source_target_pairs={{4,8},{8,4},{12,16},{16,12},{20,24},{24,20},{28,32},{32,28},{36,40... | collective-permute-start | bytes 147464 | tf_op jit(solution)/shard_map/ppermute | solution.py:230
  48.7 1.9 %collective-permute-start.3 = (bf16[96,256]{1,0:T(8,128)(2,1)S(1)}, bf16[96,256]{1,0:T(8,128)(2,1)S(1)}, u32[]{:S(2)}, u32[]{:S(2)}) collective-permute-start(bf16[96,256]{1,0:T(8,128)(2,1)S(1)} %get-tuple-element.27), channel_id=1, source_target_pairs={{0,4},{4,0},{8,12},{12,8},{16,20},{20,16},{24,28},{28,24},{32,36},... | collective-permute-start | bytes 147464 | tf_op jit(solution)/shard_map/ppermute | solution.py:230
  50.6 2.1 %shard_map.108 = (f32[12,96,256]{2,1,0:T(8,128)S(1)}, bf16[14,96,256]{2,1,0:T(8,128)(2,1)S(1)}) custom-call(s32[5,12]{1,0:T(8,128)S(1)} %bitcast.26, bf16[14,96,256]{2,1,0:T(8,128)(2,1)S(1)} %get-tuple-element.28.ext_ref, f32[12,96,256]{2,1,0:T(8,128)S(1)} %get-tuple-element.23.load_ref, f32[12,96,256]{2,1,0:T(8,128)S(1)} %get-tuple-element.24.lam_ref, ...), custom_call_target="tpu_custom_call" | custom-call | flops 2000000000 | bytes 4000000 | tf_op jit(solution)/shard_map/pallas_call | solution.py:272
  52.8 0.0 collective-permute-done.2.from_other
  52.8 0.0 collective-permute-done.3.from_partner
  52.8 2.9 %shard_map.109 = (bf16[12,96,256]{2,1,0:T(8,128)(2,1)}, f32[1,12]{1,0:T(1,128)S(1)}, bf16[14,96,256]{2,1,0:T(8,128)(2,1)S(1)}) custom-call(s32[1]{0:T(128)} %bitcast.1.parity_ref, s32[5,12]{1,0:T(8,128)S(1)} %bitcast.27, bf16[96,256]{1,0:T(8,128)(2,1)S(1)} %collective-permute-done.2.from_other, ...), custom_call_target="tpu_custom_call", output_to_operand_aliasing={{2}: (10, {})} | custom-call | flops 1000000 | bytes 4000000 | tf_op jit(solution)/shard_map/pallas_call | solution.py:277
  55.7 11.0 %psum.7 = f32[12]{0:T(128)} all-reduce(f32[12]{0:T(128)S(1)} %bitcast.28), channel_id=1, replica_groups=mesh['sub'=128,'freq'=4] {'freq'}, use_global_device_ids=true, to_apply=%region_0.0 | all-reduce | flops 12 | bytes 96 | tf_op jit(solution)/shard_map/psum | solution.py:289
  (9 shorter events, 0.0 us)
Async XLA Ops:
  0.6 34.3 %copy-start.1 = (bf16[1,12,2,96,96]{4,3,2,1,0:T(8,128)(2,1)S(1)}, bf16[1,12,2,96,96]{4,3,2,1,0:T(8,128)(2,1)}, u32[]{:S(2)}) copy-start(bf16[1,12,2,96,96]{4,3,2,1,0:T(8,128)(2,1)} %param.16) | copy-start | bytes 1327108
  0.6 34.3 %copy-start.3 = (bf16[1,12,96,256]{3,2,1,0:T(8,128)(2,1)S(1)}, bf16[1,12,96,256]{3,2,1,0:T(8,128)(2,1)}, u32[]{:S(2)}) copy-start(bf16[1,12,96,256]{3,2,1,0:T(8,128)(2,1)} %param.9) | copy-start | bytes 1769476
  1.4 0.8 %copy-start.4 = (bf16[1,96,256]{2,1,0:T(8,128)(2,1)S(1)}, bf16[1,96,256]{2,1,0:T(8,128)(2,1)}, u32[]{:S(2)}) copy-start(bf16[1,96,256]{2,1,0:T(8,128)(2,1)} %param.10) | copy-start | bytes 147460
  2.7 37.7 %copy-start.6 = (bf16[12,96,96]{2,1,0:T(8,128)(2,1)S(1)}, bf16[12,96,96]{2,1,0:T(8,128)(2,1)}, u32[]{:S(2)}) copy-start(bf16[12,96,96]{2,1,0:T(8,128)(2,1)} %stiff_ref.1) | copy-start | bytes 663556
  35.9 7.5 %collective-permute-start = (bf16[96,256]{1,0:T(8,128)(2,1)S(1)}, bf16[96,256]{1,0:T(8,128)(2,1)S(1)}, u32[]{:S(2)}, u32[]{:S(2)}) collective-permute-start(bf16[96,256]{1,0:T(8,128)(2,1)S(1)} %get-tuple-element.20), channel_id=1, source_target_pairs={{4,8},{8,4},{12,16},{16,12},{20,24},{24,20},{28,32},{32,28},{36,40... | collective-permute-start | bytes 147464 | tf_op jit(solution)/shard_map/ppermute | solution.py:230
  37.9 5.6 %collective-permute-start.1 = (bf16[96,256]{1,0:T(8,128)(2,1)S(1)}, bf16[96,256]{1,0:T(8,128)(2,1)S(1)}, u32[]{:S(2)}, u32[]{:S(2)}) collective-permute-start(bf16[96,256]{1,0:T(8,128)(2,1)S(1)} %get-tuple-element.21), channel_id=1, source_target_pairs={{0,4},{4,0},{8,12},{12,8},{16,20},{20,16},{24,28},{28,24},{32,36},... | collective-permute-start | bytes 147464 | tf_op jit(solution)/shard_map/ppermute | solution.py:230
  40.5 3.0 %copy-start = (bf16[1,12,5,2,96,96]{5,4,3,2,1,0:T(8,128)(2,1)S(1)}, bf16[1,12,5,2,96,96]{5,4,3,2,1,0:T(8,128)(2,1)}, u32[]{:S(2)}) copy-start(bf16[1,12,5,2,96,96]{5,4,3,2,1,0:T(8,128)(2,1)} %param.14) | copy-start | bytes 6635524
  40.5 3.0 %copy-start.2 = (bf16[1,12,2,96,96]{4,3,2,1,0:T(8,128)(2,1)S(1)}, bf16[1,12,2,96,96]{4,3,2,1,0:T(8,128)(2,1)}, u32[]{:S(2)}) copy-start(bf16[1,12,2,96,96]{4,3,2,1,0:T(8,128)(2,1)} %param.13) | copy-start | bytes 1327108
  40.5 3.0 %copy-start.5 = (s32[12,5]{0,1:T(8,128)S(1)}, s32[12,5]{0,1:T(8,128)}, u32[]{:S(2)}) copy-start(s32[12,5]{0,1:T(8,128)} %param.15) | copy-start | bytes 724
  44.6 8.1 %collective-permute-start.2 = (bf16[96,256]{1,0:T(8,128)(2,1)S(1)}, bf16[96,256]{1,0:T(8,128)(2,1)S(1)}, u32[]{:S(2)}, u32[]{:S(2)}) collective-permute-start(bf16[96,256]{1,0:T(8,128)(2,1)S(1)} %get-tuple-element.26), channel_id=1, source_target_pairs={{4,8},{8,4},{12,16},{16,12},{20,24},{24,20},{28,32},{32,28},{36,40... | collective-permute-start | bytes 147464 | tf_op jit(solution)/shard_map/ppermute | solution.py:230
  48.7 4.1 %collective-permute-start.3 = (bf16[96,256]{1,0:T(8,128)(2,1)S(1)}, bf16[96,256]{1,0:T(8,128)(2,1)S(1)}, u32[]{:S(2)}, u32[]{:S(2)}) collective-permute-start(bf16[96,256]{1,0:T(8,128)(2,1)S(1)} %get-tuple-element.27), channel_id=1, source_target_pairs={{0,4},{4,0},{8,12},{12,8},{16,20},{20,16},{24,28},{28,24},{32,36},... | collective-permute-start | bytes 147464 | tf_op jit(solution)/shard_map/ppermute | solution.py:230

commit v4 on v3

--- a/solution.py
+++ b/solution.py
@@ -8,7 +8,8 @@
 from jax.experimental.pallas import tpu as pltpu
 from jax.sharding import PartitionSpec as P
 
-SLOTS = 4
+SLOTS = 3
+CODE = 2048
 VMEM_LIMIT = 16 * 1024 * 1024
 
 F32 = jnp.float32
@@ -34,38 +35,53 @@
     return split_product(jnp.dot(stacked(tile_pair), block, preferred_element_type=F32))
 
 
-def pack_kernel(rows_per, code_ref, measured_ref, out_ref):
+def pack_kernel(
+    rows_per, owner_hbm, row_hbm, measured_hbm, out_ref, owner_ref, row_ref, measured_ref, sems
+):
+    copies = [
+        pltpu.make_async_copy(source, target, sems.at[i])
+        for i, (source, target) in enumerate(
+            ((owner_hbm, owner_ref), (row_hbm, row_ref), (measured_hbm, measured_ref))
+        )
+    ]
+    for copy in copies:
+        copy.start()
+    for copy in copies[:2]:
+        copy.wait()
     count = measured_ref.shape[0]
-    slots_all = out_ref.shape[0]
-    code = code_ref[...]
-    owner = code.astype(jnp.int32) >> 11
+    owner = owner_ref[...]
+    code = (owner * CODE + row_ref[...]).astype(F32)
     lanes = jnp.broadcast_to(jnp.pad(code, ((0, 0), (0, 128 - count))), (128, 128))
-    code_col = jnp.transpose(lanes)[:count, :count].astype(jnp.int32)
-    owner_col = code_col >> 11
-    row_col = code_col & 2047
+    code_col = jnp.transpose(lanes)[:count].astype(jnp.int32)
+    owner_col = code_col[:, :count] // CODE
+    row_wide = code_col & (CODE - 1)
     same = jnp.broadcast_to(owner, (count, count)) == owner_col
     sub = iota((count, count), 0)
     lane = iota((count, count), 1)
     rank_row = jnp.sum(jnp.where(same & (sub < lane), 1, 0), axis=0, keepdims=True)
     rank_col = jnp.sum(jnp.where(same & (lane < sub), 1, 0), axis=1, keepdims=True)
-    place = iota((slots_all, count), 0)
-    here = (place >> 2) == owner
-    slot = place & 3
-    pick = jnp.where(here & (slot == rank_row), 1.0, 0.0).astype(BF16)
-    tell = jnp.where(here & (slot == SLOTS - 1), 1.0, 0.0).astype(BF16)
     width = iota((count, 128), 1)
-    row_wide = jnp.broadcast_to(row_col[:, :1], (count, 128))
     block = row_wide // rows_per
     inner = row_wide - block * rows_per
-    numbers = jnp.where(width == rank_col, block + 1, 0) + jnp.where(
-        width == rank_col + SLOTS, inner, 0
-    )
+    numbers = jnp.where(width == rank_col, block + 1, 0)
+    numbers += jnp.where(width == rank_col + SLOTS, inner, 0)
     numbers = numbers.astype(F32).astype(BF16)
-    rows = jnp.dot(pick, measured_ref[...], preferred_element_type=F32)
+    place = iota((out_ref.shape[0], count), 0)
+    here = (place >> 1) == owner
+    first_half = (place & 1) == 0
+    copies[2].wait()
+    tell = jnp.where(here & first_half, 1.0, 0.0).astype(BF16)
     told = jnp.dot(tell, numbers, preferred_element_type=F32)
-    half = rows.shape[-1] // 2
-    out_ref[:, :half] = (rows[:, :half] + told).astype(BF16)
-    out_ref[:, half:] = rows[:, half:].astype(BF16)
+    out_ref[:, SLOTS * 128 :] = told.astype(BF16)
+    low, high = measured_ref[:, :128], measured_ref[:, 128:]
+    for s in range(SLOTS):
+        mine = here & (rank_row == s)
+        pick_low = jnp.where(mine & first_half, 1.0, 0.0).astype(BF16)
+        pick_high = jnp.where(mine & ~first_half, 1.0, 0.0).astype(BF16)
+        out_ref[:, s * 128 : (s + 1) * 128] = (
+            jnp.dot(pick_low, low, preferred_element_type=F32)
+            + jnp.dot(pick_high, high, preferred_element_type=F32)
+        ).astype(BF16)
 
 
 def send_edges(parity, first, last, other_ref, partner_ref):
@@ -100,21 +116,34 @@
     return loads
 
 
-def edge_kernel(parity_ref, recv_ref, resp_ref, prec_ref, place_ref, other_ref, partner_ref):
+def unpack(recv_ref, place_ref, rows_ref, line_ref):
+    peers, width = recv_ref.shape[0] // 2, recv_ref.shape[1] // (SLOTS + 1)
+    m = place_ref.shape[0]
+    line_ref[...] = recv_ref[:, SLOTS * width :].astype(F32)
+    numbers = jnp.transpose(line_ref[pl.ds(0, peers, stride=2), :]).astype(BF16)
+    lane = iota((m, width), 1)
+    for s in range(SLOTS):
+        weights = jnp.where(lane == s, m, 0) + jnp.where(lane == s + SLOTS, 1, 0)
+        told = jnp.dot(weights.astype(F32).astype(BF16), numbers, preferred_element_type=F32)
+        place_ref[:, s * peers : (s + 1) * peers] = (
+            told.astype(jnp.int32) - m - iota((m, peers), 0)
+        )
+        line_ref[...] = recv_ref[:, s * width : (s + 1) * width].astype(F32)
+        for i in range(2):
+            rows_ref[s * peers : (s + 1) * peers, i * width : (i + 1) * width] = line_ref[
+                pl.ds(i, peers, stride=2), :
+            ].astype(BF16)
+
+
+def edge_kernel(
+    parity_ref, recv_ref, resp_ref, prec_ref, place_ref, rows_ref, other_ref, partner_ref,
+    line_ref,
+):
     nb, m, cols = resp_ref.shape
     half = cols // 2
-    places = recv_ref.shape[0]
-    recv = recv_ref[...]
-    turned = jnp.transpose(recv[:, :half].astype(F32)).astype(BF16)
-    lane = iota((m, half), 1)
-    slot = iota((m, places), 1) & 3
-    where_row = jnp.full((m, places), -1.0, F32)
-    for s in range(SLOTS - 1):
-        weights = jnp.where(lane == s, m, 0) + jnp.where(lane == s + SLOTS, 1, 0)
-        told = jnp.dot(weights.astype(F32).astype(BF16), turned, preferred_element_type=F32)
-        told = pltpu.roll(told, places + s - (SLOTS - 1), 1)
-        where_row = jnp.where(slot == s, told - m, where_row)
-    place_ref[...] = where_row.astype(jnp.int32) - iota((m, places), 0)
+    unpack(recv_ref, place_ref, rows_ref, line_ref)
+    recv = rows_ref[...]
+    places = recv.shape[0]
     ones = jnp.ones((places, half), BF16)
     edges = []
     for b in (0, nb - 1):
@@ -183,29 +212,23 @@
 
 def last_kernel(
     scale, parity_ref, cols_ref, from_other, from_partner, load_ref, lam_ref, diag_ref, off_ref,
-    prec_ref, stiff_ref, _, adj_out, grad_out, ext_ref, adj_ref, part_ref, sems,
+    prec_ref, stiff_ref, _, adj_out, grad_out, ext_ref, part_ref,
 ):
     nb, m, cols = load_ref.shape
     half = cols // 2
     take_edges(parity_ref[0], from_other, from_partner, ext_ref)
     part_ref[...] = jnp.zeros_like(part_ref)
-    copies = []
     tiles = (diag_ref, off_ref, prec_ref)
     for b, lam in sweep_blocks(range(nb), cols_ref, ext_ref, load_ref, lam_ref, *tiles):
-        adj_ref[b] = lam.astype(BF16)
-        copies.append(pltpu.make_async_copy(adj_ref.at[b], adj_out.at[b], sems.at[b]))
-        copies[-1].start()
+        adj_out[b] = lam.astype(BF16)
         terms = lam * stiff_ref[b]
         part_ref[b : b + 1] = jnp.sum(terms[:, :half] + terms[:, half:], axis=0, keepdims=True)
     total = jnp.sum(jnp.transpose(part_ref[...]), axis=0, keepdims=True)
     grad_out[...] = total[:, :nb] * scale
-    for copy in copies:
-        copy.wait()
 
 
 IN_VMEM = pl.BlockSpec(memory_space=pltpu.VMEM)
 IN_SMEM = pl.BlockSpec(memory_space=pltpu.SMEM)
-IN_HBM = pl.BlockSpec(memory_space=pltpu.HBM)
 
 
 def call(kernel, outs, ins, out_specs=None, scratch=(), aliases=None, mflops=1):
@@ -239,28 +262,35 @@
     peers = lax.axis_size("sub")
     sensors = sensor_owner.shape[0]
     shape = jax.ShapeDtypeStruct
-    code = (sensor_owner * 2048 + sensor_row).astype(F32).reshape(1, sensors)
-    place_id = lax.axis_index("sub") & 1
+    owner, row = sensor_owner.reshape(1, sensors), sensor_row.reshape(1, sensors)
+    owner, row, rows_in, place_id = lax.optimization_barrier(
+        (owner, row, measured[0], lax.axis_index("sub") & 1)
+    )
     near = block_cols.T
-    code, place_id = lax.optimization_barrier((code, place_id))
+    numbers = pltpu.VMEM((1, sensors), jnp.int32)
     (packed,) = call(
-        functools.partial(pack_kernel, m), (shape((peers * SLOTS, cols), BF16),), [IN_VMEM] * 2
-    )(code, measured[0])
-    recv = lax.all_to_all(packed.reshape(peers, SLOTS, cols), "sub", 0, 0, tiled=True)
-    recv = recv.reshape(peers * SLOTS, cols)
+        functools.partial(pack_kernel, m),
+        (shape((2 * peers, (SLOTS + 1) * cols // 2), BF16),),
+        [pl.BlockSpec(memory_space=pltpu.HBM)] * 3,
+        scratch=[numbers, numbers, pltpu.VMEM((sensors, cols), BF16), pltpu.SemaphoreType.DMA((3,))],
+    )(*(pltpu.with_memory_space_constraint(x, pltpu.HBM) for x in (owner, row, rows_in)))
+    recv = lax.all_to_all(
+        packed.reshape(peers, 2, -1), "sub", 0, 0, tiled=True
+    ).reshape(packed.shape)
     parity = place_id.astype(jnp.int32).reshape(1)
 
     whole32, whole16 = shape((nb, m, cols), F32), shape((nb, m, cols), BF16)
     wide16, edge = shape((nb + 2, m, cols), BF16), shape((m, cols), BF16)
-    place, to_other, to_partner = call(
+    place, rows, to_other, to_partner = call(
         edge_kernel,
-        (shape((m, peers * SLOTS), jnp.int32), edge, edge),
+        (shape((m, peers * SLOTS), jnp.int32), shape((peers * SLOTS, cols), BF16), edge, edge),
         [IN_SMEM] + [IN_VMEM] * 3,
+        scratch=[pltpu.VMEM((2 * peers, cols // 2), F32)],
     )(parity, recv, resp, prec)
     from_other, from_partner = swap_edges(to_other, to_partner, "sub")
     load, lam, ext, stiff_resp = call(
         load_kernel, (whole32, whole32, wide16, whole32), [IN_VMEM] * 5, mflops=2000
-    )(place, recv, resp, prec, stiff_deriv)
+    )(place, rows, resp, prec, stiff_deriv)
 
     ext, to_other, to_partner = call(
         sweep_edge_kernel,
@@ -278,12 +308,7 @@
         functools.partial(last_kernel, scale),
         (whole16, shape((1, nb), F32), wide16),
         [IN_SMEM] * 2 + [IN_VMEM] * 9,
-        out_specs=(IN_HBM, IN_VMEM, IN_VMEM),
-        scratch=[
-            pltpu.VMEM((nb, m, cols), BF16),
-            pltpu.VMEM((128, 128), F32),
-            pltpu.SemaphoreType.DMA((nb,)),
-        ],
+        scratch=[pltpu.VMEM((128, 128), F32)],
         aliases={10: 2},
     )(parity, near, from_other, from_partner, load, lam, diag, off, prec, stiff_resp, ext)
     gradient = lax.psum(grad.reshape(nb), "freq")

time: 67 us -> 66.2 us (0.988)
  other arithmetic: 0.77 us -> 0 us
  local copies, waits for them, and re-layouts: 0.96 us -> 0.24 us
  Pallas kernels: 9.18 us -> 9.87 us
    unnamed x14 -> x12, local copies, waits for them, and re-layouts: 0.83 us -> 0.03 us
    reshape x1 -> x0, other arithmetic: 0.77 us -> none  [shards(): code = (sensor_owner * 2048 + sensor_row).astype(F32).reshape(1, sensors)]
where the time goes in v4:
time: 66.2 us; the launch traced here: 65.9 us
  blocking collectives  43 us (65%)
  starting transfers between devices  10.5 us (16%)
  Pallas kernels  9.87 us (15%)
  waiting for transfers between devices  1.5 us (2%)
  between operations  0.81 us (1%)
    all_to_all x1, blocking collectives, shards(): lax.all_to_all(packed.reshape(peers, 2, -1), 'sub', 0, 0, tiled=True)  32.1 us
    psum x1, blocking collectives, shards(): gradient = lax.psum(grad.reshape(nb), 'freq')  11 us
    ppermute x2, starting transfers between devices, swap_edges(): lax.ppermute(to_other, axis, others)  5.97 us
    ppermute x2, starting transfers between devices, swap_edges(): lax.ppermute(to_partner, axis, pairs)  4.5 us
    pallas_call x1, Pallas kernels, shards(): call(functools.partial(last_kernel, scale), (whole16, shape((1, nb), F32)...  3.01 us
    pallas_call x1, Pallas kernels, shards(): call(sweep_kernel, (whole32, wide16), [IN_SMEM] + [IN_VMEM] * 6, mflops=2...  2.14 us
    ppermute x2, waiting for transfers between devices, swap_edges(): lax.ppermute(to_other, axis, others)  1.49 us
    pallas_call x1, Pallas kernels, shards(): call(load_kernel, (whole32, whole32, wide16, whole32), [IN_VMEM] * 5, mfl...  1.46 us
  transfers between devices with their start and end apart: 4, of which 1 were waited for; matrix products, arithmetic and copies ran while one was open for 0% of the time, Pallas kernels for 5%

profile of v4, /device:TPU:8, one launch (start us, length us, event | category | flops | bytes accessed | tf_op | source)
XLA Modules:
  0.0 65.9 jit_solution(4316675472770152426)
XLA Ops:
  0.6 0.0 copy-start.1
  0.6 0.0 copy-start.3
  0.7 1.3 %shard_map.104 = bf16[256,512]{1,0:T(8,128)(2,1)S(1)} custom-call(s32[1,96]{1,0:T(1,128)} %bitcast.29, s32[1,96]{1,0:T(1,128)} %bitcast.30, bf16[96,256]{1,0:T(8,128)(2,1)} %bitcast.28), custom_call_target="tpu_custom_call" | custom-call | flops 1000000 | bytes 4000000 | tf_op jit(solution)/shard_map/pallas_call | solution.py:271
  2.0 0.1 reshape.25
  2.1 0.0 copy-start.5
  2.1 32.1 %all_to_all.5 = bf16[128,2,512]{2,1,0:T(2,128)(2,1)S(1)} all-to-all(bf16[128,2,512]{2,1,0:T(2,128)(2,1)S(1)} %reshape.25), channel_id=1, replica_groups=mesh['sub'=128,'freq'=4] {'sub'}, dimensions={0} | all-to-all | bytes 524288 | tf_op jit(solution)/shard_map/all_to_all | solution.py:277
  34.2 0.1 reshape.26.recv_ref
  34.3 0.8 %shard_map.105 = (s32[96,384]{1,0:T(8,128)S(1)}, bf16[384,256]{1,0:T(8,128)(2,1)S(1)}, bf16[96,256]{1,0:T(8,128)(2,1)S(1)}, bf16[96,256]{1,0:T(8,128)(2,1)S(1)}) custom-call(s32[1]{0:T(128)} %bitcast.3.parity_ref, bf16[256,512]{1,0:T(8,128)(2,1)S(1)} %reshape.26.recv_ref, bf16[12,96,256]{2,1,0:T(8,128)(2,1)S(1)} %bitcast.22, bf16[12,2,96,96]{3,2,1,0:T(8,128)(2,1)S(1)} %bitcast.14), custom_call_target="tpu_custom_call" | custom-call | flops 1000000 | bytes 4000000 | tf_op jit(solution)/shard_map/pallas_call | solution.py:284
  35.1 1.9 %collective-permute-start = (bf16[96,256]{1,0:T(8,128)(2,1)S(1)}, bf16[96,256]{1,0:T(8,128)(2,1)S(1)}, u32[]{:S(2)}, u32[]{:S(2)}) collective-permute-start(bf16[96,256]{1,0:T(8,128)(2,1)S(1)} %get-tuple-element.25), channel_id=1, source_target_pairs={{4,8},{8,4},{12,16},{16,12},{20,24},{24,20},{28,32},{32,28},{36,40... | collective-permute-start | bytes 147464 | tf_op jit(solution)/shard_map/ppermute | solution.py:253
  37.0 2.6 %collective-permute-start.1 = (bf16[96,256]{1,0:T(8,128)(2,1)S(1)}, bf16[96,256]{1,0:T(8,128)(2,1)S(1)}, u32[]{:S(2)}, u32[]{:S(2)}) collective-permute-start(bf16[96,256]{1,0:T(8,128)(2,1)S(1)} %get-tuple-element.26), channel_id=1, source_target_pairs={{0,4},{4,0},{8,12},{12,8},{16,20},{20,16},{24,28},{28,24},{32,36},... | collective-permute-start | bytes 147464 | tf_op jit(solution)/shard_map/ppermute | solution.py:253
  39.6 0.0 copy-start
  39.6 0.0 copy-start.2
  39.6 0.0 copy-start.4
  39.7 1.5 %shard_map.106 = (f32[12,96,256]{2,1,0:T(8,128)S(1)}, f32[12,96,256]{2,1,0:T(8,128)S(1)}, bf16[14,96,256]{2,1,0:T(8,128)(2,1)S(1)}, f32[12,96,256]{2,1,0:T(8,128)S(1)}) custom-call(s32[96,384]{1,0:T(8,128)S(1)} %get-tuple-element.27.place_ref, bf16[384,256]{1,0:T(8,128)(2,1)S(1)} %get-tuple-element.28.recv_ref, bf16[12,96,256]{2,1,0:T(8,128)(2,1)S(1)} %bitcast.23, ...), custom_call_target="tpu_custom_call" | custom-call | flops 2000000000 | bytes 4000000 | tf_op jit(solution)/shard_map/pallas_call | solution.py:291
  41.1 1.5 %collective-permute-done.from_other = bf16[96,256]{1,0:T(8,128)(2,1)S(1)} collective-permute-done((bf16[96,256]{1,0:T(8,128)(2,1)S(1)}, bf16[96,256]{1,0:T(8,128)(2,1)S(1)}, u32[]{:S(2)}, u32[]{:S(2)}) %collective-permute-start) | collective-permute-done | bytes 49184 | tf_op jit(solution)/shard_map/ppermute | solution.py:253
  42.6 0.0 collective-permute-done.1.from_partner
  42.6 1.2 %shard_map.107 = (bf16[14,96,256]{2,1,0:T(8,128)(2,1)S(1)}, bf16[96,256]{1,0:T(8,128)(2,1)S(1)}, bf16[96,256]{1,0:T(8,128)(2,1)S(1)}) custom-call(s32[1]{0:T(128)} %bitcast.3.parity_ref, s32[5,12]{1,0:T(8,128)S(1)} %bitcast.24, bf16[96,256]{1,0:T(8,128)(2,1)S(1)} %collective-permute-done.from_other, ...), custom_call_target="tpu_custom_call", output_to_operand_aliasing={{0}: (9, {})} | custom-call | flops 1000000 | bytes 4000000 | tf_op jit(solution)/shard_map/pallas_call | solution.py:295
  43.8 4.0 %collective-permute-start.2 = (bf16[96,256]{1,0:T(8,128)(2,1)S(1)}, bf16[96,256]{1,0:T(8,128)(2,1)S(1)}, u32[]{:S(2)}, u32[]{:S(2)}) collective-permute-start(bf16[96,256]{1,0:T(8,128)(2,1)S(1)} %get-tuple-element.32), channel_id=1, source_target_pairs={{4,8},{8,4},{12,16},{16,12},{20,24},{24,20},{28,32},{32,28},{36,40... | collective-permute-start | bytes 147464 | tf_op jit(solution)/shard_map/ppermute | solution.py:253
  47.8 1.9 %collective-permute-start.3 = (bf16[96,256]{1,0:T(8,128)(2,1)S(1)}, bf16[96,256]{1,0:T(8,128)(2,1)S(1)}, u32[]{:S(2)}, u32[]{:S(2)}) collective-permute-start(bf16[96,256]{1,0:T(8,128)(2,1)S(1)} %get-tuple-element.33), channel_id=1, source_target_pairs={{0,4},{4,0},{8,12},{12,8},{16,20},{20,16},{24,28},{28,24},{32,36},... | collective-permute-start | bytes 147464 | tf_op jit(solution)/shard_map/ppermute | solution.py:253
  49.8 2.1 %shard_map.108 = (f32[12,96,256]{2,1,0:T(8,128)S(1)}, bf16[14,96,256]{2,1,0:T(8,128)(2,1)S(1)}) custom-call(s32[5,12]{1,0:T(8,128)S(1)} %bitcast.25, bf16[14,96,256]{2,1,0:T(8,128)(2,1)S(1)} %get-tuple-element.34.ext_ref, f32[12,96,256]{2,1,0:T(8,128)S(1)} %get-tuple-element.29.load_ref, f32[12,96,256]{2,1,0:T(8,128)S(1)} %get-tuple-element.30.lam_ref, ...), custom_call_target="tpu_custom_call" | custom-call | flops 2000000000 | bytes 4000000 | tf_op jit(solution)/shard_map/pallas_call | solution.py:302
  51.9 0.0 collective-permute-done.2.from_other
  51.9 0.0 collective-permute-done.3.from_partner
  51.9 3.0 %shard_map.109 = (bf16[12,96,256]{2,1,0:T(8,128)(2,1)}, f32[1,12]{1,0:T(1,128)S(1)}, bf16[14,96,256]{2,1,0:T(8,128)(2,1)S(1)}) custom-call(s32[1]{0:T(128)} %bitcast.3.parity_ref, s32[5,12]{1,0:T(8,128)S(1)} %bitcast.26, bf16[96,256]{1,0:T(8,128)(2,1)S(1)} %collective-permute-done.2.from_other, ...), custom_call_target="tpu_custom_call", output_to_operand_aliasing={{2}: (10, {})} | custom-call | flops 1000000 | bytes 4000000 | tf_op jit(solution)/shard_map/pallas_call | solution.py:307
  55.0 11.0 %psum.7 = f32[12]{0:T(128)} all-reduce(f32[12]{0:T(128)S(1)} %bitcast.27), channel_id=1, replica_groups=mesh['sub'=128,'freq'=4] {'freq'}, use_global_device_ids=true, to_apply=%region_0.0 | all-reduce | flops 12 | bytes 96 | tf_op jit(solution)/shard_map/psum | solution.py:314
  (6 shorter events, 0.0 us)
Async XLA Ops:
  0.6 33.6 %copy-start.1 = (bf16[1,12,2,96,96]{4,3,2,1,0:T(8,128)(2,1)S(1)}, bf16[1,12,2,96,96]{4,3,2,1,0:T(8,128)(2,1)}, u32[]{:S(2)}) copy-start(bf16[1,12,2,96,96]{4,3,2,1,0:T(8,128)(2,1)} %param.16) | copy-start | bytes 1327108
  0.6 33.6 %copy-start.3 = (bf16[1,12,96,256]{3,2,1,0:T(8,128)(2,1)S(1)}, bf16[1,12,96,256]{3,2,1,0:T(8,128)(2,1)}, u32[]{:S(2)}) copy-start(bf16[1,12,96,256]{3,2,1,0:T(8,128)(2,1)} %param.9) | copy-start | bytes 1769476
  2.1 37.5 %copy-start.5 = (bf16[12,96,96]{2,1,0:T(8,128)(2,1)S(1)}, bf16[12,96,96]{2,1,0:T(8,128)(2,1)}, u32[]{:S(2)}) copy-start(bf16[12,96,96]{2,1,0:T(8,128)(2,1)} %stiff_ref.1) | copy-start | bytes 663556
  35.1 7.5 %collective-permute-start = (bf16[96,256]{1,0:T(8,128)(2,1)S(1)}, bf16[96,256]{1,0:T(8,128)(2,1)S(1)}, u32[]{:S(2)}, u32[]{:S(2)}) collective-permute-start(bf16[96,256]{1,0:T(8,128)(2,1)S(1)} %get-tuple-element.25), channel_id=1, source_target_pairs={{4,8},{8,4},{12,16},{16,12},{20,24},{24,20},{28,32},{32,28},{36,40... | collective-permute-start | bytes 147464 | tf_op jit(solution)/shard_map/ppermute | solution.py:253
  37.0 5.6 %collective-permute-start.1 = (bf16[96,256]{1,0:T(8,128)(2,1)S(1)}, bf16[96,256]{1,0:T(8,128)(2,1)S(1)}, u32[]{:S(2)}, u32[]{:S(2)}) collective-permute-start(bf16[96,256]{1,0:T(8,128)(2,1)S(1)} %get-tuple-element.26), channel_id=1, source_target_pairs={{0,4},{4,0},{8,12},{12,8},{16,20},{20,16},{24,28},{28,24},{32,36},... | collective-permute-start | bytes 147464 | tf_op jit(solution)/shard_map/ppermute | solution.py:253
  39.6 3.0 %copy-start = (bf16[1,12,5,2,96,96]{5,4,3,2,1,0:T(8,128)(2,1)S(1)}, bf16[1,12,5,2,96,96]{5,4,3,2,1,0:T(8,128)(2,1)}, u32[]{:S(2)}) copy-start(bf16[1,12,5,2,96,96]{5,4,3,2,1,0:T(8,128)(2,1)} %param.14) | copy-start | bytes 6635524
  39.6 3.0 %copy-start.2 = (bf16[1,12,2,96,96]{4,3,2,1,0:T(8,128)(2,1)S(1)}, bf16[1,12,2,96,96]{4,3,2,1,0:T(8,128)(2,1)}, u32[]{:S(2)}) copy-start(bf16[1,12,2,96,96]{4,3,2,1,0:T(8,128)(2,1)} %param.13) | copy-start | bytes 1327108
  39.6 3.0 %copy-start.4 = (s32[12,5]{0,1:T(8,128)S(1)}, s32[12,5]{0,1:T(8,128)}, u32[]{:S(2)}) copy-start(s32[12,5]{0,1:T(8,128)} %param.15) | copy-start | bytes 724
  43.8 8.1 %collective-permute-start.2 = (bf16[96,256]{1,0:T(8,128)(2,1)S(1)}, bf16[96,256]{1,0:T(8,128)(2,1)S(1)}, u32[]{:S(2)}, u32[]{:S(2)}) collective-permute-start(bf16[96,256]{1,0:T(8,128)(2,1)S(1)} %get-tuple-element.32), channel_id=1, source_target_pairs={{4,8},{8,4},{12,16},{16,12},{20,24},{24,20},{28,32},{32,28},{36,40... | collective-permute-start | bytes 147464 | tf_op jit(solution)/shard_map/ppermute | solution.py:253
  47.8 4.1 %collective-permute-start.3 = (bf16[96,256]{1,0:T(8,128)(2,1)S(1)}, bf16[96,256]{1,0:T(8,128)(2,1)S(1)}, u32[]{:S(2)}, u32[]{:S(2)}) collective-permute-start(bf16[96,256]{1,0:T(8,128)(2,1)S(1)} %get-tuple-element.33), channel_id=1, source_target_pairs={{0,4},{4,0},{8,12},{12,8},{16,20},{20,16},{24,28},{28,24},{32,36},... | collective-permute-start | bytes 147464 | tf_op jit(solution)/shard_map/ppermute | solution.py:253

commit v5 on v4

--- a/solution.py
+++ b/solution.py
@@ -295,11 +295,11 @@
     ext, to_other, to_partner = call(
         sweep_edge_kernel,
         (wide16, edge, edge),
-        [IN_SMEM] * 2 + [IN_VMEM] * 8,
+        [IN_SMEM, IN_VMEM] + [IN_VMEM] * 8,
         aliases={9: 0},
     )(parity, near, from_other, from_partner, load, lam, diag, off, prec, ext)
     from_other, from_partner = swap_edges(to_other, to_partner, "sub")
-    lam, ext = call(sweep_kernel, (whole32, wide16), [IN_SMEM] + [IN_VMEM] * 6, mflops=2000)(
+    lam, ext = call(sweep_kernel, (whole32, wide16), [IN_VMEM] + [IN_VMEM] * 6, mflops=2000)(
         near, ext, load, lam, diag, off, prec
     )
 
@@ -307,7 +307,7 @@
     adjoint, grad, _ = call(
         functools.partial(last_kernel, scale),
         (whole16, shape((1, nb), F32), wide16),
-        [IN_SMEM] * 2 + [IN_VMEM] * 9,
+        [IN_SMEM, IN_VMEM] + [IN_VMEM] * 9,
         scratch=[pltpu.VMEM((128, 128), F32)],
         aliases={10: 2},
     )(parity, near, from_other, from_partner, load, lam, diag, off, prec, stiff_resp, ext)

time: 66.2 us -> 64.7 us (0.977)
  Pallas kernels: 9.87 us -> 8.35 us
    pallas_call x2, Pallas kernels: 3.29 us -> 2.27 us  [the longest x1 1.67 us: shards(): call(sweep_kernel, (whole32, wide16), [IN_VMEM] + [IN_VMEM] * 6, mflops=2...]
where the time goes in v5:
time: 64.7 us; the launch traced here: 64.4 us
  blocking collectives  43 us (66%)
  starting transfers between devices  10.5 us (16%)
  Pallas kernels  8.35 us (13%)
  waiting for transfers between devices  1.5 us (2%)
  between operations  0.81 us (1%)
    all_to_all x1, blocking collectives, shards(): lax.all_to_all(packed.reshape(peers, 2, -1), 'sub', 0, 0, tiled=True)  32.1 us
    psum x1, blocking collectives, shards(): gradient = lax.psum(grad.reshape(nb), 'freq')  11 us
    ppermute x2, starting transfers between devices, swap_edges(): lax.ppermute(to_other, axis, others)  5.97 us
    ppermute x2, starting transfers between devices, swap_edges(): lax.ppermute(to_partner, axis, pairs)  4.5 us
    pallas_call x1, Pallas kernels, shards(): call(functools.partial(last_kernel, scale), (whole16, shape((1, nb), F32)...  2.51 us
    pallas_call x1, Pallas kernels, shards(): call(sweep_kernel, (whole32, wide16), [IN_VMEM] + [IN_VMEM] * 6, mflops=2...  1.67 us
    ppermute x2, waiting for transfers between devices, swap_edges(): lax.ppermute(to_other, axis, others)  1.49 us
    pallas_call x1, Pallas kernels, shards(): call(load_kernel, (whole32, whole32, wide16, whole32), [IN_VMEM] * 5, mfl...  1.46 us
  transfers between devices with their start and end apart: 4, of which 1 were waited for; matrix products, arithmetic and copies ran while one was open for 0% of the time, Pallas kernels for 5%

profile of v5, /device:TPU:8, one launch (start us, length us, event | category | flops | bytes accessed | tf_op | source)
XLA Modules:
  0.0 64.4 jit_solution(1831702931693156682)
XLA Ops:
  0.7 1.3 %shard_map.104 = bf16[256,512]{1,0:T(8,128)(2,1)S(1)} custom-call(s32[1,96]{1,0:T(1,128)} %bitcast.29, s32[1,96]{1,0:T(1,128)} %bitcast.30, bf16[96,256]{1,0:T(8,128)(2,1)} %bitcast.28), custom_call_target="tpu_custom_call" | custom-call | flops 1000000 | bytes 4000000 | tf_op jit(solution)/shard_map/pallas_call | solution.py:271
  2.0 0.1 reshape.25
  2.1 0.0 copy-start.5
  2.1 32.1 %all_to_all.5 = bf16[128,2,512]{2,1,0:T(2,128)(2,1)S(1)} all-to-all(bf16[128,2,512]{2,1,0:T(2,128)(2,1)S(1)} %reshape.25), channel_id=1, replica_groups=mesh['sub'=128,'freq'=4] {'sub'}, dimensions={0} | all-to-all | bytes 524288 | tf_op jit(solution)/shard_map/all_to_all | solution.py:277
  34.2 0.1 reshape.26.recv_ref
  34.3 0.8 %shard_map.105 = (s32[96,384]{1,0:T(8,128)S(1)}, bf16[384,256]{1,0:T(8,128)(2,1)S(1)}, bf16[96,256]{1,0:T(8,128)(2,1)S(1)}, bf16[96,256]{1,0:T(8,128)(2,1)S(1)}) custom-call(s32[1]{0:T(128)} %bitcast.3.parity_ref, bf16[256,512]{1,0:T(8,128)(2,1)S(1)} %reshape.26.recv_ref, bf16[12,96,256]{2,1,0:T(8,128)(2,1)S(1)} %bitcast.22, bf16[12,2,96,96]{3,2,1,0:T(8,128)(2,1)S(1)} %bitcast.14), custom_call_target="tpu_custom_call" | custom-call | flops 1000000 | bytes 4000000 | tf_op jit(solution)/shard_map/pallas_call | solution.py:284
  35.1 1.9 %collective-permute-start = (bf16[96,256]{1,0:T(8,128)(2,1)S(1)}, bf16[96,256]{1,0:T(8,128)(2,1)S(1)}, u32[]{:S(2)}, u32[]{:S(2)}) collective-permute-start(bf16[96,256]{1,0:T(8,128)(2,1)S(1)} %get-tuple-element.25), channel_id=1, source_target_pairs={{4,8},{8,4},{12,16},{16,12},{20,24},{24,20},{28,32},{32,28},{36,40... | collective-permute-start | bytes 147464 | tf_op jit(solution)/shard_map/ppermute | solution.py:253
  37.0 2.6 %collective-permute-start.1 = (bf16[96,256]{1,0:T(8,128)(2,1)S(1)}, bf16[96,256]{1,0:T(8,128)(2,1)S(1)}, u32[]{:S(2)}, u32[]{:S(2)}) collective-permute-start(bf16[96,256]{1,0:T(8,128)(2,1)S(1)} %get-tuple-element.26), channel_id=1, source_target_pairs={{0,4},{4,0},{8,12},{12,8},{16,20},{20,16},{24,28},{28,24},{32,36},... | collective-permute-start | bytes 147464 | tf_op jit(solution)/shard_map/ppermute | solution.py:253
  39.6 0.0 copy-start
  39.6 0.0 copy-start.2
  39.6 0.0 copy-start.4
  39.7 1.5 %shard_map.106 = (f32[12,96,256]{2,1,0:T(8,128)S(1)}, f32[12,96,256]{2,1,0:T(8,128)S(1)}, bf16[14,96,256]{2,1,0:T(8,128)(2,1)S(1)}, f32[12,96,256]{2,1,0:T(8,128)S(1)}) custom-call(s32[96,384]{1,0:T(8,128)S(1)} %get-tuple-element.27.place_ref, bf16[384,256]{1,0:T(8,128)(2,1)S(1)} %get-tuple-element.28.recv_ref, bf16[12,96,256]{2,1,0:T(8,128)(2,1)S(1)} %bitcast.23, ...), custom_call_target="tpu_custom_call" | custom-call | flops 2000000000 | bytes 4000000 | tf_op jit(solution)/shard_map/pallas_call | solution.py:291
  41.1 1.5 %collective-permute-done.from_other = bf16[96,256]{1,0:T(8,128)(2,1)S(1)} collective-permute-done((bf16[96,256]{1,0:T(8,128)(2,1)S(1)}, bf16[96,256]{1,0:T(8,128)(2,1)S(1)}, u32[]{:S(2)}, u32[]{:S(2)}) %collective-permute-start) | collective-permute-done | bytes 49184 | tf_op jit(solution)/shard_map/ppermute | solution.py:253
  42.6 0.0 collective-permute-done.1.from_partner
  42.6 0.0 copy-done.2
  42.6 0.0 copy-done.4
  42.6 0.6 shard_map.107
  43.2 4.0 %collective-permute-start.2 = (bf16[96,256]{1,0:T(8,128)(2,1)S(1)}, bf16[96,256]{1,0:T(8,128)(2,1)S(1)}, u32[]{:S(2)}, u32[]{:S(2)}) collective-permute-start(bf16[96,256]{1,0:T(8,128)(2,1)S(1)} %get-tuple-element.32), channel_id=1, source_target_pairs={{4,8},{8,4},{12,16},{16,12},{20,24},{24,20},{28,32},{32,28},{36,40... | collective-permute-start | bytes 147464 | tf_op jit(solution)/shard_map/ppermute | solution.py:253
  47.3 1.9 %collective-permute-start.3 = (bf16[96,256]{1,0:T(8,128)(2,1)S(1)}, bf16[96,256]{1,0:T(8,128)(2,1)S(1)}, u32[]{:S(2)}, u32[]{:S(2)}) collective-permute-start(bf16[96,256]{1,0:T(8,128)(2,1)S(1)} %get-tuple-element.33), channel_id=1, source_target_pairs={{0,4},{4,0},{8,12},{12,8},{16,20},{20,16},{24,28},{28,24},{32,36},... | collective-permute-start | bytes 147464 | tf_op jit(solution)/shard_map/ppermute | solution.py:253
  49.2 1.7 %shard_map.108 = (f32[12,96,256]{2,1,0:T(8,128)S(1)}, bf16[14,96,256]{2,1,0:T(8,128)(2,1)S(1)}) custom-call(s32[5,12]{1,0:T(8,128)S(1)} %bitcast.25, bf16[14,96,256]{2,1,0:T(8,128)(2,1)S(1)} %get-tuple-element.34.ext_ref, f32[12,96,256]{2,1,0:T(8,128)S(1)} %get-tuple-element.29.load_ref, f32[12,96,256]{2,1,0:T(8,128)S(1)} %get-tuple-element.30.lam_ref, ...), custom_call_target="tpu_custom_call" | custom-call | flops 2000000000 | bytes 4000000 | tf_op jit(solution)/shard_map/pallas_call | solution.py:302
  50.9 0.0 collective-permute-done.2.from_other
  50.9 0.0 collective-permute-done.3.from_partner
  50.9 2.5 %shard_map.109 = (bf16[12,96,256]{2,1,0:T(8,128)(2,1)}, f32[1,12]{1,0:T(1,128)S(1)}, bf16[14,96,256]{2,1,0:T(8,128)(2,1)S(1)}) custom-call(s32[1]{0:T(128)} %bitcast.3.parity_ref, s32[5,12]{1,0:T(8,128)S(1)} %bitcast.26, bf16[96,256]{1,0:T(8,128)(2,1)S(1)} %collective-permute-done.2.from_other, ...), custom_call_target="tpu_custom_call", output_to_operand_aliasing={{2}: (10, {})} | custom-call | flops 1000000 | bytes 4000000 | tf_op jit(solution)/shard_map/pallas_call | solution.py:307
  53.4 11.0 %psum.7 = f32[12]{0:T(128)} all-reduce(f32[12]{0:T(128)S(1)} %bitcast.27), channel_id=1, replica_groups=mesh['sub'=128,'freq'=4] {'freq'}, use_global_device_ids=true, to_apply=%region_0.0 | all-reduce | flops 12 | bytes 96 | tf_op jit(solution)/shard_map/psum | solution.py:314
  (6 shorter events, 0.0 us)
Async XLA Ops:
  0.6 33.6 %copy-start.1 = (bf16[1,12,2,96,96]{4,3,2,1,0:T(8,128)(2,1)S(1)}, bf16[1,12,2,96,96]{4,3,2,1,0:T(8,128)(2,1)}, u32[]{:S(2)}) copy-start(bf16[1,12,2,96,96]{4,3,2,1,0:T(8,128)(2,1)} %param.16) | copy-start | bytes 1327108
  0.6 33.6 %copy-start.3 = (bf16[1,12,96,256]{3,2,1,0:T(8,128)(2,1)S(1)}, bf16[1,12,96,256]{3,2,1,0:T(8,128)(2,1)}, u32[]{:S(2)}) copy-start(bf16[1,12,96,256]{3,2,1,0:T(8,128)(2,1)} %param.9) | copy-start | bytes 1769476
  2.1 37.5 %copy-start.5 = (bf16[12,96,96]{2,1,0:T(8,128)(2,1)S(1)}, bf16[12,96,96]{2,1,0:T(8,128)(2,1)}, u32[]{:S(2)}) copy-start(bf16[12,96,96]{2,1,0:T(8,128)(2,1)} %stiff_ref.1) | copy-start | bytes 663556
  35.1 7.5 %collective-permute-start = (bf16[96,256]{1,0:T(8,128)(2,1)S(1)}, bf16[96,256]{1,0:T(8,128)(2,1)S(1)}, u32[]{:S(2)}, u32[]{:S(2)}) collective-permute-start(bf16[96,256]{1,0:T(8,128)(2,1)S(1)} %get-tuple-element.25), channel_id=1, source_target_pairs={{4,8},{8,4},{12,16},{16,12},{20,24},{24,20},{28,32},{32,28},{36,40... | collective-permute-start | bytes 147464 | tf_op jit(solution)/shard_map/ppermute | solution.py:253
  37.0 5.6 %collective-permute-start.1 = (bf16[96,256]{1,0:T(8,128)(2,1)S(1)}, bf16[96,256]{1,0:T(8,128)(2,1)S(1)}, u32[]{:S(2)}, u32[]{:S(2)}) collective-permute-start(bf16[96,256]{1,0:T(8,128)(2,1)S(1)} %get-tuple-element.26), channel_id=1, source_target_pairs={{0,4},{4,0},{8,12},{12,8},{16,20},{20,16},{24,28},{28,24},{32,36},... | collective-permute-start | bytes 147464 | tf_op jit(solution)/shard_map/ppermute | solution.py:253
  39.6 3.0 %copy-start = (bf16[1,12,5,2,96,96]{5,4,3,2,1,0:T(8,128)(2,1)S(1)}, bf16[1,12,5,2,96,96]{5,4,3,2,1,0:T(8,128)(2,1)}, u32[]{:S(2)}) copy-start(bf16[1,12,5,2,96,96]{5,4,3,2,1,0:T(8,128)(2,1)} %param.14) | copy-start | bytes 6635524
  39.6 3.0 %copy-start.2 = (bf16[1,12,2,96,96]{4,3,2,1,0:T(8,128)(2,1)S(1)}, bf16[1,12,2,96,96]{4,3,2,1,0:T(8,128)(2,1)}, u32[]{:S(2)}) copy-start(bf16[1,12,2,96,96]{4,3,2,1,0:T(8,128)(2,1)} %param.13) | copy-start | bytes 1327108
  39.6 3.0 %copy-start.4 = (s32[12,5]{0,1:T(8,128)S(1)}, s32[12,5]{0,1:T(8,128)}, u32[]{:S(2)}) copy-start(s32[12,5]{0,1:T(8,128)} %param.15) | copy-start | bytes 724
  43.2 7.7 %collective-permute-start.2 = (bf16[96,256]{1,0:T(8,128)(2,1)S(1)}, bf16[96,256]{1,0:T(8,128)(2,1)S(1)}, u32[]{:S(2)}, u32[]{:S(2)}) collective-permute-start(bf16[96,256]{1,0:T(8,128)(2,1)S(1)} %get-tuple-element.32), channel_id=1, source_target_pairs={{4,8},{8,4},{12,16},{16,12},{20,24},{24,20},{28,32},{32,28},{36,40... | collective-permute-start | bytes 147464 | tf_op jit(solution)/shard_map/ppermute | solution.py:253
  47.3 3.6 %collective-permute-start.3 = (bf16[96,256]{1,0:T(8,128)(2,1)S(1)}, bf16[96,256]{1,0:T(8,128)(2,1)S(1)}, u32[]{:S(2)}, u32[]{:S(2)}) collective-permute-start(bf16[96,256]{1,0:T(8,128)(2,1)S(1)} %get-tuple-element.33), channel_id=1, source_target_pairs={{0,4},{4,0},{8,12},{12,8},{16,20},{20,16},{24,28},{28,24},{32,36},... | collective-permute-start | bytes 147464 | tf_op jit(solution)/shard_map/ppermute | solution.py:253
